TPU v7x, 32 devices: a whole 2x2x4 slice. The times are simulated.
32 devices in a mesh: parts: 2 (over y), tile: 4 (over z), src: 2 (over x), focus: 2 (over core).
Axes of the slice: x: 2, y: 2, z: 4, core: 2. Of those that a mesh axis runs over, the one named last changes fastest.
Arguments:
- mask: float32 [768, 1536], P('parts', 'tile'), parts along dimension 0, may hold values from -1 to 1
- target: float32 [768, 1536], P('parts', 'tile'), parts along dimension 0, may hold values from 0 to 1
- pupil: float32 [2, 16, 4, 64, 64], P(None, 'src', 'focus'), may hold values from -6 to 6
- weights: float32 [16], P('src'), may hold values from 0.25 to 4
- counts: int32 [8], P('parts'), parts along dimension 0, may hold values from 1 to 4, as said below
Outputs:
- gradient: float32 [768, 1536], P(('parts', 'src', 'focus'), 'tile'), parts along dimension 0
There are 2 independent parts, one for each index of `parts`. A program takes and returns all parts, laid end to end along the dimension named above; an argument that names none is the same for every part. Nothing has to cross between parts.
Inputs may be any that keep to these rules, and one draw needn't show every extreme that they name: Corners 0 to counts - 1 of a subtile are in use; of the two subtiles t and t + 2 at least one uses a single corner; some subtile uses all 4.
All inputs are finite; a program needn't handle non-finite values.
Results may differ from a plain program's by a relative error of at most 0.0003.
Values sent between devices are 32-bit elements; how exact they have to be, the bound alone decides.
No kernel may reach another device: no remote copies, remote signals or barrier semaphores. Data moves between devices by JAX's collectives and lax.ppermute only.
A program may use at most 128 MiB of HBM per device.

v0:
```python
import math

import jax
import jax.numpy as jnp
from jax import lax
from jax.sharding import PartitionSpec as P

AMBIT = 64


resist_slope = 4.0
resist_level = 0.5


def with_halo(block, sides, width):
    for axis, dim in sides:
        count = lax.axis_size(axis)
        forward = [(i, i + 1) for i in range(count - 1)]
        backward = [(target, source) for source, target in forward]
        low = lax.ppermute(
            lax.slice_in_dim(block, block.shape[dim] - width, None, axis=dim), axis, forward
        )
        high = lax.ppermute(lax.slice_in_dim(block, 0, width, axis=dim), axis, backward)
        block = jnp.concatenate([low, block, high], axis=dim)
    return block


def passed_along(value, axis, by):
    peers = lax.axis_size(axis)
    pairs = [(i, i + by) for i in range(peers) if 0 <= i + by < peers]
    return lax.ppermute(value, axis, pairs)


def product(left, right):
    return jnp.dot(left, right, precision=lax.Precision.HIGHEST, preferred_element_type=jnp.float32)


def phase_table(freqs, length, offset, count):
    kvalues = jnp.arange(freqs, dtype=jnp.int32) - freqs // 2
    nvalues = jnp.arange(count, dtype=jnp.int32) + offset
    phase = jnp.mod(kvalues[:, None] * nvalues[None, :], length).astype(jnp.float32) * (
        2.0 * math.pi / length
    )
    return (jnp.cos(phase), jnp.sin(phase))


def add_edges(window_grad, width, tile, from_left, from_right):
    filler = jnp.zeros((window_grad.shape[0], tile - width), jnp.float32)
    middle = window_grad[:, width : width + tile]
    middle = middle + jnp.concatenate([from_left, filler], axis=1)
    return middle + jnp.concatenate([filler, from_right], axis=1)


def per_device(mask, target, pupil, weights, counts):
    tile = mask.shape[0]
    freqs = pupil.shape[-1]
    width = AMBIT
    win = tile + 2 * width
    local_src = weights.shape[0]
    sources = local_src * lax.axis_size("src")
    corner_dev = pupil.shape[2]
    norm_win = 1.0 / math.sqrt(win)
    norm_back = math.sqrt(2.0 / freqs)
    cos_col, sin_col = phase_table(freqs, win, 0, win)
    col_re = cos_col * norm_win
    col_im = -sin_col * norm_win
    cos_row, sin_row = phase_table(freqs, win, width, tile)
    row_re = cos_row * norm_win
    row_im = -sin_row * norm_win
    back_re = cos_row.T * norm_back
    back_im = sin_row.T * norm_back
    back_re_t = cos_row * norm_back
    back_im_t = sin_row * norm_back
    src_scale = weights / sources
    extended = with_halo(mask, (("tile", 1),), width)
    x_re = product(extended, col_re.T)
    x_im = product(extended, col_im.T)
    spec_re = product(row_re, x_re) - product(row_im, x_im)
    spec_im = product(row_re, x_im) + product(row_im, x_re)
    tile_index = lax.axis_index("tile")
    focus_index = lax.axis_index("focus")
    own_load = jnp.clip(counts[tile_index] - focus_index * corner_dev, 0, corner_dev)
    pup_re = pupil[0]
    pup_im = pupil[1]
    zero_int = jnp.zeros((), jnp.int32)
    source_count = jnp.asarray(local_src, jnp.int32)

    def fields(g_re, g_im):
        h_re = product(g_re, back_re_t) - product(g_im, back_im_t)
        h_im = product(g_re, back_im_t) + product(g_im, back_re_t)
        e_re = product(back_re, h_re) - product(back_im, h_im)
        e_im = product(back_re, h_im) + product(back_im, h_re)
        return (e_re, e_im)

    keeps = []
    for corner in range(corner_dev):
        keeps.append(
            jnp.where(
                corner < own_load - 1,
                source_count,
                jnp.where(corner == own_load - 1, source_count, zero_int),
            )
        )
    store_shape = (corner_dev * local_src, tile, tile)
    stores = (jnp.zeros(store_shape, jnp.float32), jnp.zeros(store_shape, jnp.float32))
    offsets = []
    offset = zero_int
    partials = []
    for corner in range(corner_dev):
        offsets.append(offset)
        forward_corner_re = pup_re[:, corner]
        forward_corner_im = pup_im[:, corner]

        def forward_add_source(source, carry):
            total, store_re, store_im = carry
            p_re = lax.dynamic_index_in_dim(forward_corner_re, source, 0, keepdims=False)
            p_im = lax.dynamic_index_in_dim(forward_corner_im, source, 0, keepdims=False)
            e_re, e_im = fields(p_re * spec_re - p_im * spec_im, p_re * spec_im + p_im * spec_re)
            place = offset + source
            store_re = lax.dynamic_update_index_in_dim(store_re, e_re, place, 0)
            store_im = lax.dynamic_update_index_in_dim(store_im, e_im, place, 0)
            return (total + src_scale[source] * (e_re * e_re + e_im * e_im), store_re, store_im)

        start = (jnp.zeros((tile, tile), jnp.float32), stores[0], stores[1])
        total, store_re, store_im = lax.fori_loop(
            zero_int, keeps[corner], forward_add_source, start
        )
        total, stores = (total, (store_re, store_im))
        partials.append(total)
        offset = offset + keeps[corner]
    partials = jnp.stack(partials)
    actives = (jnp.arange(corner_dev, dtype=jnp.int32) < own_load).astype(jnp.float32)
    summed = lax.psum(partials, "src")
    resist = jax.nn.sigmoid(resist_slope * (summed - resist_level))
    slopes = (
        2.0
        * (resist - target[None])
        * resist_slope
        * resist
        * (1.0 - resist)
        * actives[:, None, None]
    )
    gs_re = jnp.zeros((freqs, freqs), jnp.float32)
    gs_im = jnp.zeros((freqs, freqs), jnp.float32)
    for corner in range(corner_dev):
        corner_re = pup_re[:, corner]
        corner_im = pup_im[:, corner]
        adjoint_offset = offsets[corner]
        slope = slopes[corner]

        def adjoint_add_source(source, carry):
            place = adjoint_offset + source
            e_re = lax.dynamic_index_in_dim(stores[0], place, 0, keepdims=False)
            e_im = lax.dynamic_index_in_dim(stores[1], place, 0, keepdims=False)
            p_re = lax.dynamic_index_in_dim(corner_re, source, 0, keepdims=False)
            p_im = lax.dynamic_index_in_dim(corner_im, source, 0, keepdims=False)
            factor = 2.0 * src_scale[source] * slope
            ge_re = factor * e_re
            ge_im = factor * e_im
            gh_re = product(back_re_t, ge_re) + product(back_im_t, ge_im)
            gh_im = product(back_re_t, ge_im) - product(back_im_t, ge_re)
            gg_re = product(gh_re, back_re) + product(gh_im, back_im)
            gg_im = product(gh_im, back_re) - product(gh_re, back_im)
            return (carry[0] + p_re * gg_re + p_im * gg_im, carry[1] + p_re * gg_im - p_im * gg_re)

        empty = jnp.zeros((freqs, freqs), jnp.float32)
        part_re, part_im = lax.fori_loop(
            zero_int, keeps[corner], adjoint_add_source, (empty, empty)
        )
        gs_re = gs_re + part_re
        gs_im = gs_im + part_im
    gx_re = product(row_re.T, gs_re) + product(row_im.T, gs_im)
    gx_im = product(row_re.T, gs_im) - product(row_im.T, gs_re)
    window_grad = product(gx_re, col_re) + product(gx_im, col_im)
    from_right = passed_along(window_grad[:, :width], "tile", -1)
    from_left = passed_along(window_grad[:, width + tile :], "tile", 1)
    middle = add_edges(window_grad, width, tile, from_left, from_right)
    return lax.psum_scatter(middle, ("src", "focus"), scatter_dimension=0, tiled=True)


def solution(mesh):
    return jax.shard_map(
        per_device,
        mesh=mesh,
        in_specs=(
            P("parts", "tile"),
            P("parts", "tile"),
            P(None, "src", "focus", None, None),
            P("src"),
            P("parts"),
        ),
        out_specs=P(("parts", "src", "focus"), "tile"),
        check_vma=False,
    )
```

profile of v0, /device:TPU:0, one launch (start us, length us, event | category | flops | bytes accessed | tf_op | source)
XLA Modules:
  0.0 543.7 jit_solution(12759937555417626799)
XLA Ops:
  7.7 5.0 collective-permute-start
  18.1 2.9 collective-permute-done.1
  20.9 2.5 fusion.315
  24.1 2.5 fusion.316
  28.7 4.6 broadcast.89
  33.3 4.7 broadcast.89.clone
  38.0 97.6 %while.64 = (s32[]{:T(128)}, f32[384,384]{0,1:T(8,128)S(1)}, f32[16,384,384]{1,2,0:T(8,128)}, f32[16,384,384]{1,2,0:T(8,128)}, s32[]{:T(128)}, /*index=5*/f32[8]...) while((s32[]{:T(128)}, f32[384,384]{0,1:T(8,128)S(1)}, ...), condition=%wide.region_1.2_spmd.clone.clone.clone, body=%wide.region_0.1_spmd.clone.clone.clone.sunk | while | flops 532537344 | bytes 8239340 | solution.py:125
  47.1 2.5 fusion.505
  59.3 2.5 fusion.505
  71.5 2.5 fusion.505
  83.6 2.5 fusion.505
  95.8 2.5 fusion.505
  108.0 2.5 fusion.505
  120.2 2.5 fusion.505
  132.3 2.5 fusion.505
  135.7 96.8 %while.65 = (s32[]{:T(128)}, f32[384,384]{0,1:T(8,128)S(1)}, f32[16,384,384]{1,2,0:T(8,128)}, f32[16,384,384]{1,2,0:T(8,128)}, s32[]{:T(128)}, /*index=5*/f32[8]...) while((s32[]{:T(128)}, f32[384,384]{0,1:T(8,128)S(1)}, ...), condition=%wide.region_3.4_spmd.clone.clone.clone, body=%wide.region_2.3_spmd.clone.clone.clone.sunk | while | flops 532537344 | bytes 8239369 | solution.py:125
  234.2 9.7 %copy.10 = f32[16,384,384]{2,1,0:T(8,128)} copy(f32[16,384,384]{1,2,0:T(8,128)} %get-tuple-element.891) | data formatting | bytes 18874368
  243.9 9.7 %copy.11 = f32[16,384,384]{2,1,0:T(8,128)} copy(f32[16,384,384]{1,2,0:T(8,128)} %get-tuple-element.892) | data formatting | bytes 18874368
  253.6 23.9 %all-reduce.4.cloned.1.call-done = f32[2,384,384]{2,1,0:T(8,128)} async-done(((f32[2,384,384]{2,1,0:T(8,128)}), f32[2,384,384]{2,1,0:T(8,128)}) %all-reduce.4.cloned.1.call-update) | async-done | bytes 1179664 | tf_op jit(solution)/shard_map/psum | solution.py:133
  279.4 109.3 %while.67 = (s32[]{:T(128)}, f32[64,64]{1,0:T(8,128)S(1)}, f32[64,64]{1,0:T(8,128)S(1)}, s32[]{:T(128)}, f32[8,64,64]{2,1,0:T(8,128)S(1)}, /*index=5*/f32[8]{0:T...) while((s32[]{:T(128)}, f32[64,64]{1,0:T(8,128)S(1)}, ...), condition=%wide.region_8.9_spmd.clone.clone.clone, body=%wide.region_7.8_spmd.clone.clone.clone.sunk | while | flops 532701184 | bytes 5914913 | solution.py:167
  388.7 109.2 %while.66 = (s32[]{:T(128)}, f32[64,64]{1,0:T(8,128)S(1)}, f32[64,64]{1,0:T(8,128)S(1)}, s32[]{:T(128)}, f32[8,64,64]{2,1,0:T(8,128)S(1)}, /*index=5*/f32[8]{0:T...) while((s32[]{:T(128)}, f32[64,64]{1,0:T(8,128)S(1)}, ...), condition=%wide.region_6.7_spmd.clone.clone.clone, body=%wide.region_5.6_spmd.clone.clone.clone.sunk | while | flops 532701184 | bytes 5914884 | solution.py:167
  506.8 2.9 collective-permute-done.2
  509.8 4.1 collective-permute-done.3
  515.0 21.7 %reduce-scatter.2.cloned.1.call-done = f32[96,384]{1,0:T(8,128)} async-done(((f32[384,384]{1,0:T(8,128)}), f32[96,384]{1,0:T(8,128)}) %reduce-scatter.2.cloned.1.call-update) | async-done | bytes 147472 | tf_op jit(solution)/shard_map/reduce_scatter | solution.py:178
  (355 shorter events, 401.4 us)
Async XLA Ops:
  6.5 271.0 %all-reduce.4.cloned.1.call-start = ((), (), s32[]{:S(2)}) async-start(), calls=%async_computation.1 | async-start | bytes 2359296 | tf_op jit(solution)/shard_map/psum | solution.py:133
  7.7 10.4 %collective-permute-start = (f32[384,64]{1,0:T(8,128)S(1)}, f32[384,64]{1,0:T(8,128)S(1)}, u32[]{:S(2)}, u32[]{:S(2)}) collective-permute-start(f32[384,64]{1,0:T(8,128)S(1)} %get-tuple-element.1018), channel_id=1, source_target_pairs={{0,4},{4,8},{8,12},{1,5},{5,9},{9,13},{2,6},{6,10},{10,14},{3,7},{... | collective-permute-start | bytes 294920 | tf_op jit(solution)/shard_map/ppermute | solution.py:20
  12.7 8.3 %collective-permute-start.1 = (f32[384,64]{1,0:T(8,128)S(1)}, f32[384,64]{1,0:T(8,128)S(1)}, u32[]{:S(2)}, u32[]{:S(2)}) collective-permute-start(f32[384,64]{1,0:T(8,128)S(1)} %get-tuple-element.1019), channel_id=1, source_target_pairs={{4,0},{8,4},{12,8},{5,1},{9,5},{13,9},{6,2},{10,6},{14,10},{7,3},{... | collective-permute-start | bytes 294920 | tf_op jit(solution)/shard_map/ppermute | solution.py:23
  234.2 302.5 %reduce-scatter.2.cloned.1.call-start = ((), (), s32[]{:S(2)}) async-start(), calls=%async_computation.2 | async-start | bytes 737280 | tf_op jit(solution)/shard_map/reduce_scatter | solution.py:178
  243.9 33.6 %copy-start = (f32[384,384]{1,0:T(8,128)S(1)}, f32[384,384]{1,0:T(8,128)}, u32[]{:S(2)}) copy-start(f32[384,384]{1,0:T(8,128)} %param.14) | copy-start | bytes 1769476
  504.2 5.6 %collective-permute-start.2 = (f32[384,64]{1,0:T(8,128)S(1)}, f32[384,64]{1,0:T(8,128)S(1)}, u32[]{:S(2)}, u32[]{:S(2)}) collective-permute-start(f32[384,64]{1,0:T(8,128)S(1)} %get-tuple-element.1016), channel_id=1, source_target_pairs={{0,4},{4,8},{8,12},{1,5},{5,9},{9,13},{2,6},{6,10},{10,14},{3,7},{... | collective-permute-start | bytes 294920 | tf_op jit(solution)/shard_map/ppermute | solution.py:31
  505.5 8.4 %collective-permute-start.3 = (f32[384,64]{1,0:T(8,128)S(1)}, f32[384,64]{1,0:T(8,128)S(1)}, u32[]{:S(2)}, u32[]{:S(2)}) collective-permute-start(f32[384,64]{1,0:T(8,128)S(1)} %get-tuple-element.1017), channel_id=1, source_target_pairs={{4,0},{8,4},{12,8},{5,1},{9,5},{13,9},{6,2},{10,6},{14,10},{7,3},{... | collective-permute-start | bytes 294920 | tf_op jit(solution)/shard_map/ppermute | solution.py:31
Sparse Core Ops, SparseCore 0:
  234.3 43.1 all-reduce.3
  515.1 21.4 reduce-scatter.1
where the time goes:
time: 554 us; the launch traced here: 544 us
  matrix products  378 us (68%)
  local copies, waits for them, and re-layouts  67.8 us (12%)
  waiting for transfers between devices  55.5 us (10%)
  between operations  14.5 us (3%)
  loops' own time  13.9 us (3%)
  starting transfers between devices  8.9 us (2%)
    dot_general x268, matrix products, product(): jnp.dot(left, right, precision=lax.Precision.HIGHEST, preferred_element_t...  378 us
    psum x1, waiting for transfers between devices, per_device(): summed = lax.psum(partials, 'src')  23.9 us
    reduce_scatter x1, waiting for transfers between devices, per_device(): lax.psum_scatter(middle, ('src', 'focus'), scatter_dimension=0, tiled=True)  21.7 us
    unnamed x4, local copies, waits for them, and re-layouts  19.4 us
    dynamic_update_slice x16, local copies, waits for them, and re-layouts, forward_add_source(): store_im = lax.dynamic_update_index_in_dim(store_im, e_im, place, 0)  14.1 us
    another operation x2, loops' own time, per_device(): lax.fori_loop(zero_int, keeps[corner], adjoint_add_source, (empty, empty))  12.4 us
  transfers between devices with their start and end apart: 6, of which 5 were waited for; matrix products, arithmetic and copies ran while one was open for 4% of the time, Pallas kernels for 0%

commit v1 on v0

v1 whole, which is shorter than its diff:
```python
import math

import jax
import jax.numpy as jnp
import numpy as np
from jax import lax
from jax.experimental import pallas as pl
from jax.experimental.pallas import tpu as pltpu
from jax.sharding import PartitionSpec as P

AMBIT = 64

RESIST_SLOPE = 4.0
RESIST_LEVEL = 0.5

VMEM = pl.BlockSpec(memory_space=pltpu.VMEM)
SMEM = pl.BlockSpec(memory_space=pltpu.SMEM)


def halves(value):
    value = np.asarray(value, np.float32)
    high = value.astype(jnp.bfloat16)
    low = (value - high.astype(np.float32)).astype(jnp.bfloat16)
    return np.stack([high, low])


def split(value):
    high = value.astype(jnp.bfloat16)
    low = (value - high.astype(jnp.float32)).astype(jnp.bfloat16)
    return high, low


def mm(left, right):
    return lax.dot_general(
        left, right, (((1,), (0,)), ((), ())), preferred_element_type=jnp.float32
    )


def mm3(left, right):
    lh, ll = left
    rh, rl = right
    return mm(jnp.concatenate([lh, ll, lh], axis=1), jnp.concatenate([rh, rh, rl], axis=0))


def phase(freqs, length, positions):
    k = np.arange(freqs) - freqs // 2
    angle = np.mod(k[:, None] * np.asarray(positions)[None, :], length) * (2.0 * math.pi / length)
    return np.cos(angle), np.sin(angle)


def make_tables(tile, freqs, width):
    win = tile + 2 * width
    grid = 2 * freqs
    norm_win = 1.0 / math.sqrt(win)
    norm_back = math.sqrt(2.0 / freqs)
    cos_col, sin_col = phase(freqs, win, np.arange(win))
    col_re, col_im = cos_col * norm_win, -sin_col * norm_win
    cos_row, sin_row = phase(freqs, win, np.arange(tile) + width)
    row_re, row_im = cos_row * norm_win, -sin_row * norm_win
    cos_grid, sin_grid = phase(freqs, grid, np.arange(grid))
    a_re, a_im = cos_grid.T * norm_back, sin_grid.T * norm_back

    row = np.concatenate([row_re, row_im], axis=0)
    colt = np.concatenate([col_re.T, col_im.T], axis=1)
    side = max(128, width)
    edge = np.zeros((2, side, 2 * freqs))
    edge[0, side - width :] = colt[:width]
    edge[1, :width] = colt[win - width :]

    right1 = np.block([[a_re.T, a_im.T], [-a_im.T, a_re.T]])
    left2 = np.concatenate([a_re, a_im], axis=0)
    back2 = np.concatenate([a_re.T, a_im.T], axis=0)

    q = np.arange(-(freqs - 1), freqs)
    at = (np.arange(tile) + width)[:, None] / win - np.arange(grid)[None, :] / grid
    up = np.cos(2.0 * math.pi * at[:, :, None] * q).sum(-1) / grid

    l2h, l2l = halves(left2)
    b2h, b2l = halves(back2)
    return dict(
        row=halves(row),
        colt=halves(colt[width : width + tile]),
        edge=np.stack([halves(edge[0]), halves(edge[1])]),
        right1=halves(right1),
        left2=np.concatenate([l2h, l2h, l2l], axis=1),
        back2=np.block([[b2h, b2h], [b2l, b2l]]),
        up=halves(up),
        upt=halves(up.T),
        rowt=halves(row.T),
        colown=halves(np.concatenate([col_re, col_im], 0)[:, width : width + tile]),
        coledge=np.stack([halves(edge[0].T), halves(edge[1].T)]),
    )


def swapped_halves(x):
    return pltpu.roll(x, x.shape[-1] // 2, x.ndim - 1)


def left_lanes(shape):
    return lax.broadcasted_iota(jnp.int32, shape, len(shape) - 1) < shape[-1] // 2


def as_spectrum(z):
    half = z.shape[0] // 2
    turned = swapped_halves(z[half:])
    return z[:half] + jnp.where(left_lanes(turned.shape), -turned, turned)


def pack(pupil_ref, source, corner, scale):
    re = pupil_ref[0, source, corner] * scale
    im = pupil_ref[1, source, corner] * scale
    return jnp.concatenate([re, im], axis=1)


def source_scale(weights_ref, source, sources):
    w = jnp.full((1, 1), weights_ref[source], jnp.float32)
    return jnp.sqrt(w / sources)


def send_kernel(sources, where_ref, weights_ref, pupil_ref, out_ref):
    for d in range(out_ref.shape[0]):
        for s in range(out_ref.shape[1]):
            scale = source_scale(weights_ref, s, sources)
            out_ref[d, s] = pack(pupil_ref, s, where_ref[1 + d], scale)


def edge_kernel(where_ref, mask_ref, row_ref, edge_ref, out_ref):
    side = edge_ref.shape[2]
    focus = where_ref[0]
    start = pl.multiple_of((1 - focus) * (mask_ref.shape[1] - side), 128)
    slab = split(mask_ref[:, pl.ds(start, side)])
    y = mm3((row_ref[0], row_ref[1]), slab)
    out_ref[...] = as_spectrum(mm3(split(y), (edge_ref[focus, 0], edge_ref[focus, 1])))


def own_kernel(
    sources, where_ref, weights_ref, pupil_ref, mask_ref, row_ref, colt_ref, spec_ref, pack_ref
):
    y = mm3((row_ref[0], row_ref[1]), split(mask_ref[...]))
    spec_ref[...] = as_spectrum(mm3(split(y), (colt_ref[0], colt_ref[1])))
    for s in range(pack_ref.shape[0]):
        scale = source_scale(weights_ref, s, sources)
        pack_ref[s] = pack(pupil_ref, s, where_ref[0], scale)


def forward(spec, pupil_of, count, right1_ref, left2_ref, field_ref):
    freqs, grid = spec.shape[0], right1_ref.shape[2] // 2
    turned = swapped_halves(spec)
    low = left_lanes(spec.shape)
    spec_a = jnp.where(low, spec, turned)
    spec_b = jnp.where(low, -turned, spec)
    right1 = (right1_ref[0], right1_ref[1])
    left2 = left2_ref[...]
    total = jnp.zeros((grid, grid), jnp.float32)
    for s in range(count):
        p = pupil_of(s)
        g = p * spec_a + swapped_halves(p) * spec_b
        hh, hl = split(mm3(split(g), right1))
        f = mm(left2, jnp.concatenate([hh, hl, hh], axis=0))
        e_re = f[:grid, :grid] - f[grid:, grid:]
        e_im = f[:grid, grid:] + f[grid:, :grid]
        field_ref[s, :, :grid] = e_re
        field_ref[s, :, grid:] = e_im
        total = total + (e_re * e_re + e_im * e_im)
    return total


def adjoint(intensity, target, active, pupil_of, count, right1t, back2_ref, up, upt, field_ref):
    grid = intensity.shape[0]
    freqs = grid // 2
    image = mm3(up, split(mm3(split(intensity), upt)))
    resist = jax.nn.sigmoid(RESIST_SLOPE * (image - RESIST_LEVEL))
    slope = 2.0 * (resist - target) * RESIST_SLOPE * resist * (1.0 - resist)
    down = mm3(split(mm3(upt, split(slope))), up) * (2.0 * active)
    down2 = jnp.concatenate([down, down], axis=1)
    back2 = back2_ref[...]
    th, tl = right1t
    both = jnp.concatenate([th, tl], axis=1)
    t1 = jnp.zeros((freqs, 2 * freqs), jnp.float32)
    t2 = jnp.zeros((freqs, 2 * freqs), jnp.float32)
    for s in range(count):
        eh, el = split(down2 * field_ref[s])
        f = mm(back2, jnp.concatenate([eh, el], axis=0))
        f = f[: 2 * freqs] + f[2 * freqs :]
        h = jnp.concatenate(
            [f[:freqs, :grid] + f[freqs:, grid:], f[:freqs, grid:] - f[freqs:, :grid]], axis=1
        )
        hh, hl = split(h)
        q = mm(hh, both)
        q = q[:, : 2 * freqs] + q[:, 2 * freqs :] + mm(hl, th)
        p = pupil_of(s)
        t1 = t1 + p * q
        t2 = t2 + swapped_halves(p) * q
    low = left_lanes(t1.shape)
    return jnp.where(low, t1 + swapped_halves(t1), t2 - swapped_halves(t2))


def pick(packs):
    local = packs[0].shape[0]
    return lambda s: packs[s // local][s % local]


def main_kernel(n_spec, n_pack, active_ref, *refs):
    specs, refs = refs[:n_spec], refs[n_spec:]
    packs, refs = refs[:n_pack], refs[n_pack:]
    target_ref, right1_ref, right1t_ref, left2_ref, back2_ref, up_ref, upt_ref = refs[:7]
    out_ref, field_ref = refs[7:]
    spec = sum(ref[...] for ref in specs[1:]) + specs[0][...]
    pupil_of = pick(packs)
    count = n_pack * packs[0].shape[0]
    intensity = forward(spec, pupil_of, count, right1_ref, left2_ref, field_ref)
    out_ref[...] = adjoint(
        intensity,
        target_ref[...],
        active_ref[0],
        pupil_of,
        count,
        (right1t_ref[0], right1t_ref[1]),
        back2_ref,
        (up_ref[0], up_ref[1]),
        (upt_ref[0], upt_ref[1]),
        field_ref,
    )


def forward_kernel(n_spec, n_pack, *refs):
    specs, refs = refs[:n_spec], refs[n_spec:]
    packs, refs = refs[:n_pack], refs[n_pack:]
    right1_ref, left2_ref, intensity_ref, field_ref = refs
    spec = sum(ref[...] for ref in specs[1:]) + specs[0][...]
    count = n_pack * packs[0].shape[0]
    intensity_ref[...] = forward(spec, pick(packs), count, right1_ref, left2_ref, field_ref)


def adjoint_kernel(n_part, n_pack, active_ref, *refs):
    parts, refs = refs[:n_part], refs[n_part:]
    packs, refs = refs[:n_pack], refs[n_pack:]
    target_ref, right1t_ref, back2_ref, up_ref, upt_ref, field_ref, out_ref = refs
    out_ref[...] = adjoint(
        sum(ref[...] for ref in parts[1:]) + parts[0][...],
        target_ref[...],
        active_ref[0],
        pick(packs),
        n_pack * packs[0].shape[0],
        (right1t_ref[0], right1t_ref[1]),
        back2_ref,
        (up_ref[0], up_ref[1]),
        (upt_ref[0], upt_ref[1]),
        field_ref,
    )


def final_kernel(n_own, n_near, where_ref, *refs):
    own, refs = refs[:n_own], refs[n_own:]
    near, refs = refs[:n_near], refs[n_near:]
    across_ref, rowt_ref, colown_ref, coledge_ref, out_ref = refs
    rows, tile = out_ref.shape
    side = coledge_ref.shape[3]
    focus = where_ref[0]
    start = pl.multiple_of(where_ref[1] * rows, rows)
    rowt = (rowt_ref[0, pl.ds(start, rows)], rowt_ref[1, pl.ds(start, rows)])

    def lines(gs):
        turned = swapped_halves(gs)
        stack = jnp.concatenate([gs, jnp.where(left_lanes(gs.shape), turned, -turned)], axis=0)
        return split(mm3(rowt, split(stack)))

    received = sum(ref[...] for ref in near[1:]) + near[0][...]
    across = across_ref[...]
    first = focus == 0
    from_right = jnp.where(first, received, across)
    from_left = jnp.where(first, across, received)
    main = mm3(lines(sum(ref[...] for ref in own[1:]) + own[0][...]), (colown_ref[0], colown_ref[1]))
    high = mm3(lines(from_right), (coledge_ref[0, 0], coledge_ref[0, 1]))
    low = mm3(lines(from_left), (coledge_ref[1, 0], coledge_ref[1, 1]))
    out_ref[...] = main
    out_ref[:, :side] = out_ref[:, :side] + low
    out_ref[:, tile - side :] = out_ref[:, tile - side :] + high


def call(kernel, shapes, specs, scratch=()):
    many = isinstance(shapes, (list, tuple))
    return pl.pallas_call(
        kernel,
        out_shape=[jax.ShapeDtypeStruct(s, jnp.float32) for s in shapes]
        if many
        else jax.ShapeDtypeStruct(shapes.shape, jnp.float32),
        in_specs=specs,
        out_specs=[VMEM] * len(shapes) if many else VMEM,
        scratch_shapes=list(scratch),
    )


class Shape:
    def __init__(self, *shape):
        self.shape = shape


def per_device(mask, target, pupil, weights, counts):
    tile = mask.shape[0]
    freqs = pupil.shape[-1]
    grid = 2 * freqs
    local_src = weights.shape[0]
    corner_dev = pupil.shape[2]
    n_tile, n_src, n_focus = (lax.axis_size(a) for a in ("tile", "src", "focus"))
    sources = local_src * n_src
    group = corner_dev if n_src % corner_dev == 0 else 1
    n_corner = corner_dev // group
    assert n_focus == 2
    t_index, s_index, f_index = (lax.axis_index(a) for a in ("tile", "src", "focus"))
    rank = s_index % group
    i32 = jnp.int32
    tables = {name: jnp.asarray(value) for name, value in make_tables(tile, freqs, AMBIT).items()}
    tables["right1t"] = jnp.asarray(
        np.swapaxes(np.asarray(make_tables(tile, freqs, AMBIT)["right1"]), 1, 2)
    )

    def hop_src(value, by):
        return lax.ppermute(value, "src", [(i, (i + by) % n_src) for i in range(n_src)])

    def hop_group(value, by):
        pairs = [(i, i // group * group + (i + by) % group) for i in range(n_src)]
        return lax.ppermute(value, "src", pairs)

    def hop_focus(value):
        return lax.ppermute(value, "focus", [(0, 1), (1, 0)])

    def hop_tile(value, by):
        def place(t, s, f):
            return (t * n_src + s) * n_focus + f

        pairs = []
        for t in range(n_tile - 1):
            for s in range(n_src):
                u = (s + by) % n_src
                pairs.append((place(t, s, 0), place(t + 1, u, 1)))
                pairs.append((place(t + 1, s, 1), place(t, u, 0)))
        return lax.ppermute(value, ("tile", "src", "focus"), pairs)

    got = []
    if group > 1:
        where = jnp.stack([f_index] + [(rank + d) % group for d in range(1, group)]).astype(i32)
        sends = call(
            lambda *refs: send_kernel(sources, *refs),
            Shape(group - 1, local_src, freqs, 2 * freqs),
            [SMEM, SMEM, VMEM],
        )(where, weights, pupil)
        got = [hop_group(sends[d - 1], d) for d in range(1, group)]
    edge = call(edge_kernel, Shape(freqs, 2 * freqs), [SMEM, VMEM, VMEM, VMEM])(
        jnp.stack([f_index]).astype(i32), mask, tables["row"], tables["edge"]
    )
    near = hop_tile(edge, 0)
    spec, own_pack = call(
        lambda *refs: own_kernel(sources, *refs),
        [(freqs, 2 * freqs), (local_src, freqs, 2 * freqs)],
        [SMEM, SMEM, VMEM, VMEM, VMEM, VMEM],
    )(jnp.stack([rank]).astype(i32), weights, pupil, mask, tables["row"], tables["colt"])
    specs = [spec, near, hop_focus(near)]

    gradient = []
    for c in range(n_corner):
        if group > 1:
            packs = [own_pack] + got
            corner = f_index * corner_dev + rank
        else:
            packs = [
                call(
                    lambda *refs: send_kernel(sources, *refs),
                    Shape(1, local_src, freqs, 2 * freqs),
                    [SMEM, SMEM, VMEM],
                )(jnp.array([0, c], i32), weights, pupil)[0]
            ]
            corner = f_index * corner_dev + c
        active = (corner < counts[t_index]).astype(jnp.float32)[None]
        n_pack = len(packs)
        field = (n_pack * local_src, grid, 2 * grid)
        if n_src == group:
            gs = call(
                lambda *refs: main_kernel(len(specs), n_pack, *refs),
                Shape(freqs, 2 * freqs),
                [SMEM] + [VMEM] * (len(specs) + n_pack + 7),
                [pltpu.VMEM(field, jnp.float32)],
            )(
                active,
                *specs,
                *packs,
                target,
                *(tables[k] for k in ("right1", "right1t", "left2", "back2", "up", "upt")),
            )
        else:
            part, fields = call(
                lambda *refs: forward_kernel(len(specs), n_pack, *refs),
                [(grid, grid), field],
                [VMEM] * (len(specs) + n_pack + 2),
            )(*specs, *packs, tables["right1"], tables["left2"])
            parts = [part] + [hop_src(part, r) for r in range(group, n_src, group)]
            gs = call(
                lambda *refs: adjoint_kernel(len(parts), n_pack, *refs),
                Shape(freqs, 2 * freqs),
                [SMEM] + [VMEM] * (len(parts) + n_pack + 6),
            )(
                active,
                *parts,
                *packs,
                target,
                *(tables[k] for k in ("right1t", "back2", "up", "upt")),
                fields,
            )
        gradient.append(gs)
    gs = sum(gradient[1:]) + gradient[0] if len(gradient) > 1 else gradient[0]
    gs = gs + hop_focus(gs)
    own = [gs] + [hop_src(gs, d) for d in range(1, n_src)]
    near = [hop_tile(gs, d) for d in range(n_src)]
    received = sum(near[1:]) + near[0] if len(near) > 1 else near[0]
    across = hop_focus(received)
    rows = tile // (n_src * n_focus)
    where = jnp.stack([f_index, s_index * n_focus + f_index]).astype(i32)
    return call(
        lambda *refs: final_kernel(len(own), 1, *refs),
        Shape(rows, tile),
        [SMEM] + [VMEM] * (len(own) + 5),
    )(
        where,
        *own,
        received,
        across,
        *(tables[k] for k in ("rowt", "colown", "coledge")),
    )


def solution(mesh):
    return jax.shard_map(
        per_device,
        mesh=mesh,
        in_specs=(
            P("parts", "tile"),
            P("parts", "tile"),
            P(None, "src", "focus", None, None),
            P("src"),
            P("parts"),
        ),
        out_specs=P(("parts", "src", "focus"), "tile"),
        check_vma=False,
    )
```

time: 554 us -> 44.5 us (0.08); the launches traced: 544 us -> 44.1 us
  matrix products: 378 us -> 0 us
  local copies, waits for them, and re-layouts: 67.8 us -> 2.57 us
  waiting for transfers between devices: 55.5 us -> 7.03 us
  Pallas kernels: 0 us -> 18.6 us
  loops' own time: 13.9 us -> 0 us
  between operations: 14.5 us -> 0.75 us
    dot_general x268 -> x0, matrix products: 378 us -> none  [product(): jnp.dot(left, right, precision=lax.Precision.HIGHEST, preferred_element_t...]
    psum x1 -> x0, waiting for transfers between devices: 23.9 us -> none  [per_device(): summed = lax.psum(partials, 'src')]
    reduce_scatter x1 -> x0, waiting for transfers between devices: 21.7 us -> none  [per_device(): lax.psum_scatter(middle, ('src', 'focus'), scatter_dimension=0, tiled=True)]
    dynamic_slice x33 -> x1, local copies, waits for them, and re-layouts: 21.6 us -> 0.58 us  [per_device(): active = (corner < counts[t_index]).astype(jnp.float32)[None]]
    pallas_call x0 -> x5, Pallas kernels: none -> 18.6 us  [the longest x1 9.02 us: per_device(): call(lambda *refs: main_kernel(len(specs), n_pack, *refs), Shape(freqs, 2...]
    unnamed x4 -> x16, local copies, waits for them, and re-layouts: 19.4 us -> 1.99 us
    dynamic_update_slice x16 -> x0, local copies, waits for them, and re-layouts: 14.1 us -> none  [forward_add_source(): store_im = lax.dynamic_update_index_in_dim(store_im, e_im, place, 0)]
    another operation x4 -> x0, loops' own time: 13.9 us -> none  [the longest x2 12.4 us: per_device(): lax.fori_loop(zero_int, keeps[corner], adjoint_add_source, (empty, empty))]
  transfers between devices with their start and end apart: 6 -> 8, of which waited for: 5 -> 4; matrix products, arithmetic and copies ran while one was open for 4% -> 3% of each run, Pallas kernels for 0% -> 11%
where the time goes in v1:
time: 44.5 us; the launch traced here: 44.1 us
  Pallas kernels  18.6 us (42%)
  starting transfers between devices  13.2 us (30%)
  waiting for transfers between devices  7.03 us (16%)
  local copies, waits for them, and re-layouts  2.57 us (6%)
  other arithmetic  1.92 us (4%)
  between operations  0.75 us (2%)
    pallas_call x1, Pallas kernels, per_device(): call(lambda *refs: main_kernel(len(specs), n_pack, *refs), Shape(freqs, 2...  9.02 us
    ppermute x3, starting transfers between devices, hop_tile(): return lax.ppermute(value, ('tile', 'src', 'focus'), pairs)  7.98 us
    ppermute x3, waiting for transfers between devices, hop_tile(): return lax.ppermute(value, ('tile', 'src', 'focus'), pairs)  5.36 us
    ppermute x1, starting transfers between devices, hop_group(): return lax.ppermute(value, 'src', pairs)  2.97 us
    pallas_call x1, Pallas kernels, per_device(): call(lambda *refs: own_kernel(sources, *refs), [(freqs, 2 * freqs), (loca...  2.8 us
    pallas_call x1, Pallas kernels, per_device(): call(lambda *refs: final_kernel(len(own), 1, *refs), Shape(rows, tile), [...  2.42 us
    pallas_call x1, Pallas kernels, per_device(): call(edge_kernel, Shape(freqs, 2 * freqs), [SMEM, VMEM, VMEM, VMEM])  2.25 us
    pallas_call x1, Pallas kernels, per_device(): call(lambda *refs: send_kernel(sources, *refs), Shape(group - 1, local_sr...  2.08 us
  transfers between devices with their start and end apart: 8, of which 4 were waited for; matrix products, arithmetic and copies ran while one was open for 3% of the time, Pallas kernels for 11%

profile of v1, /device:TPU:0, one launch (start us, length us, event | category | flops | bytes accessed | tf_op | source)
XLA Modules:
  0.0 44.1 jit_solution(5915821202650490283)
XLA Ops:
  0.0 0.6 %pad_add_fusion.1.refs_0_ = s32[2]{0:T(128)} fusion(s32[1]{0:T(128)} %bitcast.5, s32[1]{0:T(128)} %bitcast.where_ref), kind=kLoop, calls=%fused_computation.1 | loop fusion | flops 2 | bytes 16 | tf_op jit(solution)/shard_map/stack | solution.py:342
  0.6 2.1 %shard_map.165 = f32[1,8,64,128]{3,2,1,0:T(8,128)} custom-call(s32[2]{0:T(128)} %pad_add_fusion.1.refs_0_, f32[8]{0:T(128)} %refs_1_.3, f32[2,8,2,64,64]{4,3,2,1,0:T(8,128)} %refs_2_.3), custom_call_target="tpu_custom_call" | custom-call | tf_op jit(solution)/shard_map/pallas_call | solution.py:343
  2.6 3.0 %collective-permute-start.2 = (f32[8,64,128]{2,1,0:T(8,128)}, f32[8,64,128]{2,1,0:T(8,128)S(1)}, u32[]{:S(2)}, u32[]{:S(2)}) collective-permute-start(f32[8,64,128]{2,1,0:T(8,128)} %bitcast.7), channel_id=1, source_target_pairs={{0,2},{2,0},{1,3},{3,1},{4,6},{6,4},{5,7},{7,5},{8,10},{10,8},{9,1... | collective-permute-start | bytes 786440 | tf_op jit(solution)/shard_map/ppermute | solution.py:323
  5.6 2.3 %shard_map.164 = f32[64,128]{1,0:T(8,128)} custom-call(s32[1]{0:T(128)} %bitcast.where_ref, f32[384,384]{1,0:T(8,128)} %mask_ref.1, bf16[2,128,384]{2,1,0:T(8,128)(2,1)} %constant.52.clone.refs_4_.row_ref.refs_6_, bf16[2,2,128,128]{3,2,1,0:T(8,128)(2,1)} %constant.54.clone.edge_ref), custom_call_target="tpu_custom_call" | custom-call | tf_op jit(solution)/shard_map/pallas_call | solution.py:349
  7.9 2.6 %collective-permute-start = (f32[64,128]{1,0:T(8,128)}, f32[64,128]{1,0:T(8,128)S(1)}, u32[]{:S(2)}, u32[]{:S(2)}) collective-permute-start(f32[64,128]{1,0:T(8,128)} %shard_map.164), channel_id=1, source_target_pairs={{0,5},{5,0},{2,7},{7,2},{4,9},{9,4},{6,11},{11,6},{8,13},{13,8},{1... | collective-permute-start | bytes 98312 | tf_op jit(solution)/shard_map/ppermute | solution.py:338
  10.5 2.8 %collective-permute-done.refs_2_ = f32[64,128]{1,0:T(8,128)S(1)} collective-permute-done((f32[64,128]{1,0:T(8,128)}, f32[64,128]{1,0:T(8,128)S(1)}, u32[]{:S(2)}, u32[]{:S(2)}) %collective-permute-start) | collective-permute-done | bytes 32800 | tf_op jit(solution)/shard_map/ppermute | solution.py:338
  13.3 0.7 %copy-done.7 = s32[4]{0:T(128)S(1)} copy-done((s32[4]{0:T(128)S(1)}, s32[4]{0:T(128)}, u32[]{:S(2)}) %copy-start.7) | copy-done | bytes 40
  14.0 0.6 %dynamic_slice.3 = s32[1]{0:T(128)} dynamic-slice(s32[4]{0:T(128)S(1)} %copy-done.7, s32[]{:T(128)S(6)} %select_n.15), dynamic_slice_sizes={1} | dynamic-slice | bytes 12 | tf_op jit(solution)/shard_map/dynamic_slice | solution.py:374
  15.2 2.8 %shard_map.163 = (f32[64,128]{1,0:T(8,128)}, f32[8,64,128]{2,1,0:T(8,128)}) custom-call(s32[1]{0:T(128)} %bitcast.4.refs_0_, f32[8]{0:T(128)} %refs_1_.3, f32[2,8,2,64,64]{4,3,2,1,0:T(8,128)} %refs_2_.3, f32[384,384]{1,0:T(8,128)} %mask_ref.1, bf16[2,128,384]{2,1,0:T(8,128)(2,1)} %constant.52.clone.refs_4_.row_ref.refs_6_, ...), custom_call_target="tpu_custom_call" | custom-call | tf_op jit(solution)/shard_map/pallas_call | solution.py:353
  18.0 0.6 %copy-done.4 = f32[64,128]{1,0:T(8,128)} copy-done((f32[64,128]{1,0:T(8,128)}, f32[64,128]{1,0:T(8,128)S(1)}, u32[]{:S(2)}) %copy-start.4) | copy-done | bytes 32792
  18.6 0.1 copy-done
  18.7 9.0 %shard_map.166 = f32[64,128]{1,0:T(8,128)} custom-call(f32[1]{0:T(128)} %bitcast.3.refs_0_, f32[64,128]{1,0:T(8,128)} %get-tuple-element.7.refs_1_, f32[64,128]{1,0:T(8,128)} %copy-done.3, f32[64,128]{1,0:T(8,128)} %copy-done.4, f32[8,64,128]{2,1,0:T(8,128)} %get-tuple-element.8.refs_4_, f32[8,64,128]{2,1,0:T(8,128)} %copy-done, f32[384,384]{1,0:T(8,128)} %refs_6_.2, ...), custom_call_target="tpu_custom_call" | custom-call | tf_op jit(solution)/shard_map/pallas_call | solution.py:378
  27.7 0.5 %collective-permute-start.3 = (f32[64,128]{1,0:T(8,128)}, f32[64,128]{1,0:T(8,128)S(1)}, u32[]{:S(2)}, u32[]{:S(2)}) collective-permute-start(f32[64,128]{1,0:T(8,128)} %shard_map.166), channel_id=1, source_target_pairs={{0,1},{1,0},{2,3},{3,2},{4,5},{5,4},{6,7},{7,6},{8,9},{9,8},{10,11... | collective-permute-start | bytes 98312 | tf_op jit(solution)/shard_map/ppermute | solution.py:326
  28.2 1.1 %collective-permute-done.3 = f32[64,128]{1,0:T(8,128)S(1)} collective-permute-done((f32[64,128]{1,0:T(8,128)}, f32[64,128]{1,0:T(8,128)S(1)}, u32[]{:S(2)}, u32[]{:S(2)}) %collective-permute-start.3) | collective-permute-done | bytes 32800 | tf_op jit(solution)/shard_map/ppermute | solution.py:326
  29.3 0.8 %add.31.refs_1_ = f32[64,128]{1,0:T(8,128)S(1)} add(f32[64,128]{1,0:T(8,128)} %shard_map.166, f32[64,128]{1,0:T(8,128)S(1)} %collective-permute-done.3) | non-fusion elementwise | flops 8192 | bytes 98304 | tf_op jit(solution)/shard_map/add | solution.py:411
  30.1 3.4 %collective-permute-start.6 = (f32[64,128]{1,0:T(8,128)S(1)}, f32[64,128]{1,0:T(8,128)S(1)}, u32[]{:S(2)}, u32[]{:S(2)}) collective-permute-start(f32[64,128]{1,0:T(8,128)S(1)} %add.31.refs_1_), channel_id=1, source_target_pairs={{0,5},{5,0},{2,7},{7,2},{4,9},{9,4},{6,11},{11,6},{8,13},{13,8},{1... | collective-permute-start | bytes 98312 | tf_op jit(solution)/shard_map/ppermute | solution.py:338
  33.5 1.9 %collective-permute-start.5 = (f32[64,128]{1,0:T(8,128)S(1)}, f32[64,128]{1,0:T(8,128)S(1)}, u32[]{:S(2)}, u32[]{:S(2)}) collective-permute-start(f32[64,128]{1,0:T(8,128)S(1)} %add.31.refs_1_), channel_id=1, source_target_pairs={{0,7},{5,2},{2,5},{7,0},{4,11},{9,6},{6,9},{11,4},{8,15},{13,10},{... | collective-permute-start | bytes 98312 | tf_op jit(solution)/shard_map/ppermute | solution.py:338
  35.4 1.7 %collective-permute-start.4 = (f32[64,128]{1,0:T(8,128)S(1)}, f32[64,128]{1,0:T(8,128)S(1)}, u32[]{:S(2)}, u32[]{:S(2)}) collective-permute-start(f32[64,128]{1,0:T(8,128)S(1)} %add.31.refs_1_), channel_id=1, source_target_pairs={{0,2},{2,0},{1,3},{3,1},{4,6},{6,4},{5,7},{7,5},{8,10},{10,8},{9,1... | collective-permute-start | bytes 98312 | tf_op jit(solution)/shard_map/ppermute | solution.py:319
  37.2 2.6 %collective-permute-done.5 = f32[64,128]{1,0:T(8,128)S(1)} collective-permute-done((f32[64,128]{1,0:T(8,128)S(1)}, f32[64,128]{1,0:T(8,128)S(1)}, u32[]{:S(2)}, u32[]{:S(2)}) %collective-permute-start.5) | collective-permute-done | bytes 32800 | tf_op jit(solution)/shard_map/ppermute | solution.py:338
  39.8 0.1 collective-permute-start.7
  39.8 0.6 %pad_add_fusion.refs_0_ = s32[2]{0:T(128)} fusion(s32[1]{0:T(128)} %bitcast.1, s32[1]{0:T(128)} %bitcast.where_ref), kind=kLoop, calls=%fused_computation | loop fusion | flops 2 | bytes 16 | tf_op jit(solution)/shard_map/stack | solution.py:417
  40.4 0.6 %collective-permute-done.7.refs_4_ = f32[64,128]{1,0:T(8,128)S(1)} collective-permute-done((f32[64,128]{1,0:T(8,128)S(1)}, f32[64,128]{1,0:T(8,128)S(1)}, u32[]{:S(2)}, u32[]{:S(2)}) %collective-permute-start.7) | collective-permute-done | bytes 32800 | tf_op jit(solution)/shard_map/ppermute | solution.py:326
  41.1 0.6 %copy-done.6 = f32[64,128]{1,0:T(8,128)} copy-done((f32[64,128]{1,0:T(8,128)}, f32[64,128]{1,0:T(8,128)S(1)}, u32[]{:S(2)}) %copy-start.6) | copy-done | bytes 32792
  41.7 2.4 %shard_map.167 = f32[96,384]{1,0:T(8,128)} custom-call(s32[2]{0:T(128)} %pad_add_fusion.refs_0_, f32[64,128]{1,0:T(8,128)} %copy-done.1, f32[64,128]{1,0:T(8,128)} %copy-done.5, f32[64,128]{1,0:T(8,128)} %copy-done.2, f32[64,128]{1,0:T(8,128)} %copy-done.6, bf16[2,384,128]{2,1,0:T(8,128)(2,1)} %constant.53.clone.refs_5_, ...), custom_call_target="tpu_custom_call" | custom-call | tf_op jit(solution)/shard_map/pallas_call | solution.py:418
  (18 shorter events, 0.1 us)
Async XLA Ops:
  2.6 15.4 %collective-permute-start.2 = (f32[8,64,128]{2,1,0:T(8,128)}, f32[8,64,128]{2,1,0:T(8,128)S(1)}, u32[]{:S(2)}, u32[]{:S(2)}) collective-permute-start(f32[8,64,128]{2,1,0:T(8,128)} %bitcast.7), channel_id=1, source_target_pairs={{0,2},{2,0},{1,3},{3,1},{4,6},{6,4},{5,7},{7,5},{8,10},{10,8},{9,1... | collective-permute-start | bytes 786440 | tf_op jit(solution)/shard_map/ppermute | solution.py:323
  7.9 5.4 %collective-permute-start = (f32[64,128]{1,0:T(8,128)}, f32[64,128]{1,0:T(8,128)S(1)}, u32[]{:S(2)}, u32[]{:S(2)}) collective-permute-start(f32[64,128]{1,0:T(8,128)} %shard_map.164), channel_id=1, source_target_pairs={{0,5},{5,0},{2,7},{7,2},{4,9},{9,4},{6,11},{11,6},{8,13},{13,8},{1... | collective-permute-start | bytes 98312 | tf_op jit(solution)/shard_map/ppermute | solution.py:338
  13.3 4.7 %copy-start.3 = (f32[64,128]{1,0:T(8,128)}, f32[64,128]{1,0:T(8,128)S(1)}, u32[]{:S(2)}) copy-start(f32[64,128]{1,0:T(8,128)S(1)} %collective-permute-done.refs_2_) | copy-start | bytes 98308
  13.3 4.7 %collective-permute-start.1 = (f32[64,128]{1,0:T(8,128)S(1)}, f32[64,128]{1,0:T(8,128)S(1)}, u32[]{:S(2)}, u32[]{:S(2)}) collective-permute-start(f32[64,128]{1,0:T(8,128)S(1)} %collective-permute-done.refs_2_), channel_id=1, source_target_pairs={{0,1},{1,0},{2,3},{3,2},{4,5},{5,4},{6,7},{7,6},{8,9},{9,8},{10,11... | collective-permute-start | bytes 98312 | tf_op jit(solution)/shard_map/ppermute | solution.py:326
  13.3 0.7 %copy-start.7 = (s32[4]{0:T(128)S(1)}, s32[4]{0:T(128)}, u32[]{:S(2)}) copy-start(s32[4]{0:T(128)} %param.21) | copy-start | bytes 52
  18.0 0.6 %copy-start.4 = (f32[64,128]{1,0:T(8,128)}, f32[64,128]{1,0:T(8,128)S(1)}, u32[]{:S(2)}) copy-start(f32[64,128]{1,0:T(8,128)S(1)} %collective-permute-done.1.refs_3_) | copy-start | bytes 98308
  18.0 0.7 %copy-start = (f32[8,64,128]{2,1,0:T(8,128)}, f32[8,64,128]{2,1,0:T(8,128)S(1)}, u32[]{:S(2)}) copy-start(f32[8,64,128]{2,1,0:T(8,128)S(1)} %collective-permute-done.2.refs_5_) | copy-start | bytes 786436
  27.7 1.6 %collective-permute-start.3 = (f32[64,128]{1,0:T(8,128)}, f32[64,128]{1,0:T(8,128)S(1)}, u32[]{:S(2)}, u32[]{:S(2)}) collective-permute-start(f32[64,128]{1,0:T(8,128)} %shard_map.166), channel_id=1, source_target_pairs={{0,1},{1,0},{2,3},{3,2},{4,5},{5,4},{6,7},{7,6},{8,9},{9,8},{10,11... | collective-permute-start | bytes 98312 | tf_op jit(solution)/shard_map/ppermute | solution.py:326
  30.1 9.7 %copy-start.1 = (f32[64,128]{1,0:T(8,128)}, f32[64,128]{1,0:T(8,128)S(1)}, u32[]{:S(2)}) copy-start(f32[64,128]{1,0:T(8,128)S(1)} %add.31.refs_1_) | copy-start | bytes 98308
  30.1 7.1 %collective-permute-start.6 = (f32[64,128]{1,0:T(8,128)S(1)}, f32[64,128]{1,0:T(8,128)S(1)}, u32[]{:S(2)}, u32[]{:S(2)}) collective-permute-start(f32[64,128]{1,0:T(8,128)S(1)} %add.31.refs_1_), channel_id=1, source_target_pairs={{0,5},{5,0},{2,7},{7,2},{4,9},{9,4},{6,11},{11,6},{8,13},{13,8},{1... | collective-permute-start | bytes 98312 | tf_op jit(solution)/shard_map/ppermute | solution.py:338
  33.5 6.2 %collective-permute-start.5 = (f32[64,128]{1,0:T(8,128)S(1)}, f32[64,128]{1,0:T(8,128)S(1)}, u32[]{:S(2)}, u32[]{:S(2)}) collective-permute-start(f32[64,128]{1,0:T(8,128)S(1)} %add.31.refs_1_), channel_id=1, source_target_pairs={{0,7},{5,2},{2,5},{7,0},{4,11},{9,6},{6,9},{11,4},{8,15},{13,10},{... | collective-permute-start | bytes 98312 | tf_op jit(solution)/shard_map/ppermute | solution.py:338
  35.4 5.0 %collective-permute-start.4 = (f32[64,128]{1,0:T(8,128)S(1)}, f32[64,128]{1,0:T(8,128)S(1)}, u32[]{:S(2)}, u32[]{:S(2)}) collective-permute-start(f32[64,128]{1,0:T(8,128)S(1)} %add.31.refs_1_), channel_id=1, source_target_pairs={{0,2},{2,0},{1,3},{3,1},{4,6},{6,4},{5,7},{7,5},{8,10},{10,8},{9,1... | collective-permute-start | bytes 98312 | tf_op jit(solution)/shard_map/ppermute | solution.py:319
  39.8 1.3 %copy-start.2 = (f32[64,128]{1,0:T(8,128)}, f32[64,128]{1,0:T(8,128)S(1)}, u32[]{:S(2)}) copy-start(f32[64,128]{1,0:T(8,128)S(1)} %add.32.refs_3_) | copy-start | bytes 98308
  39.8 1.3 %collective-permute-start.7 = (f32[64,128]{1,0:T(8,128)S(1)}, f32[64,128]{1,0:T(8,128)S(1)}, u32[]{:S(2)}, u32[]{:S(2)}) collective-permute-start(f32[64,128]{1,0:T(8,128)S(1)} %add.32.refs_3_), channel_id=1, source_target_pairs={{0,1},{1,0},{2,3},{3,2},{4,5},{5,4},{6,7},{7,6},{8,9},{9,8},{10,11... | collective-permute-start | bytes 98312 | tf_op jit(solution)/shard_map/ppermute | solution.py:326
  40.4 0.6 %copy-start.5 = (f32[64,128]{1,0:T(8,128)}, f32[64,128]{1,0:T(8,128)S(1)}, u32[]{:S(2)}) copy-start(f32[64,128]{1,0:T(8,128)S(1)} %collective-permute-done.4.refs_2_) | copy-start | bytes 98308
  41.1 0.6 %copy-start.6 = (f32[64,128]{1,0:T(8,128)}, f32[64,128]{1,0:T(8,128)S(1)}, u32[]{:S(2)}) copy-start(f32[64,128]{1,0:T(8,128)S(1)} %collective-permute-done.7.refs_4_) | copy-start | bytes 98308

commit v2 on v1

--- a/solution.py
+++ b/solution.py
@@ -117,16 +117,16 @@
     return jnp.sqrt(w / sources)
 
 
-def send_kernel(sources, where_ref, weights_ref, pupil_ref, out_ref):
+def send_kernel(sources, corner_of, weights_ref, pupil_ref, out_ref):
     for d in range(out_ref.shape[0]):
         for s in range(out_ref.shape[1]):
             scale = source_scale(weights_ref, s, sources)
-            out_ref[d, s] = pack(pupil_ref, s, where_ref[1 + d], scale)
-
-
-def edge_kernel(where_ref, mask_ref, row_ref, edge_ref, out_ref):
+            out_ref[d, s] = pack(pupil_ref, s, corner_of(d), scale)
+
+
+def edge_kernel(mask_ref, row_ref, edge_ref, out_ref):
     side = edge_ref.shape[2]
-    focus = where_ref[0]
+    focus = lax.axis_index("focus")
     start = pl.multiple_of((1 - focus) * (mask_ref.shape[1] - side), 128)
     slab = split(mask_ref[:, pl.ds(start, side)])
     y = mm3((row_ref[0], row_ref[1]), slab)
@@ -134,13 +134,13 @@
 
 
 def own_kernel(
-    sources, where_ref, weights_ref, pupil_ref, mask_ref, row_ref, colt_ref, spec_ref, pack_ref
+    sources, corner_of, weights_ref, pupil_ref, mask_ref, row_ref, colt_ref, spec_ref, pack_ref
 ):
     y = mm3((row_ref[0], row_ref[1]), split(mask_ref[...]))
     spec_ref[...] = as_spectrum(mm3(split(y), (colt_ref[0], colt_ref[1])))
     for s in range(pack_ref.shape[0]):
         scale = source_scale(weights_ref, s, sources)
-        pack_ref[s] = pack(pupil_ref, s, where_ref[0], scale)
+        pack_ref[s] = pack(pupil_ref, s, corner_of(0), scale)
 
 
 def forward(spec, pupil_of, count, right1_ref, left2_ref, field_ref):
@@ -195,12 +195,17 @@
     return jnp.where(low, t1 + swapped_halves(t1), t2 - swapped_halves(t2))
 
 
+def active_here(corner_of, counts_ref):
+    used = counts_ref[lax.axis_index("tile")]
+    return (corner_of() < used).astype(jnp.float32)
+
+
 def pick(packs):
     local = packs[0].shape[0]
     return lambda s: packs[s // local][s % local]
 
 
-def main_kernel(n_spec, n_pack, active_ref, *refs):
+def main_kernel(n_spec, n_pack, corner_of, counts_ref, *refs):
     specs, refs = refs[:n_spec], refs[n_spec:]
     packs, refs = refs[:n_pack], refs[n_pack:]
     target_ref, right1_ref, right1t_ref, left2_ref, back2_ref, up_ref, upt_ref = refs[:7]
@@ -212,7 +217,7 @@
     out_ref[...] = adjoint(
         intensity,
         target_ref[...],
-        active_ref[0],
+        active_here(corner_of, counts_ref),
         pupil_of,
         count,
         (right1t_ref[0], right1t_ref[1]),
@@ -232,14 +237,14 @@
     intensity_ref[...] = forward(spec, pick(packs), count, right1_ref, left2_ref, field_ref)
 
 
-def adjoint_kernel(n_part, n_pack, active_ref, *refs):
+def adjoint_kernel(n_part, n_pack, corner_of, counts_ref, *refs):
     parts, refs = refs[:n_part], refs[n_part:]
     packs, refs = refs[:n_pack], refs[n_pack:]
     target_ref, right1t_ref, back2_ref, up_ref, upt_ref, field_ref, out_ref = refs
     out_ref[...] = adjoint(
         sum(ref[...] for ref in parts[1:]) + parts[0][...],
         target_ref[...],
-        active_ref[0],
+        active_here(corner_of, counts_ref),
         pick(packs),
         n_pack * packs[0].shape[0],
         (right1t_ref[0], right1t_ref[1]),
@@ -250,14 +255,15 @@
     )
 
 
-def final_kernel(n_own, n_near, where_ref, *refs):
+def final_kernel(n_own, n_near, *refs):
     own, refs = refs[:n_own], refs[n_own:]
     near, refs = refs[:n_near], refs[n_near:]
     across_ref, rowt_ref, colown_ref, coledge_ref, out_ref = refs
     rows, tile = out_ref.shape
     side = coledge_ref.shape[3]
-    focus = where_ref[0]
-    start = pl.multiple_of(where_ref[1] * rows, rows)
+    focus = lax.axis_index("focus")
+    strip = lax.axis_index("src") * lax.axis_size("focus") + focus
+    start = pl.multiple_of(strip * rows, rows)
     rowt = (rowt_ref[0, pl.ds(start, rows)], rowt_ref[1, pl.ds(start, rows)])
 
     def lines(gs):
@@ -278,10 +284,12 @@
     out_ref[:, tile - side :] = out_ref[:, tile - side :] + high
 
 
-def call(kernel, shapes, specs, scratch=()):
+def call(kernel, shapes, specs, scratch=(), flops=0, limit=8):
     many = isinstance(shapes, (list, tuple))
     return pl.pallas_call(
         kernel,
+        cost_estimate=pl.CostEstimate(flops=flops, bytes_accessed=1 << 20, transcendentals=0),
+        compiler_params=pltpu.CompilerParams(vmem_limit_bytes=limit << 20),
         out_shape=[jax.ShapeDtypeStruct(s, jnp.float32) for s in shapes]
         if many
         else jax.ShapeDtypeStruct(shapes.shape, jnp.float32),
@@ -307,9 +315,13 @@
     group = corner_dev if n_src % corner_dev == 0 else 1
     n_corner = corner_dev // group
     assert n_focus == 2
-    t_index, s_index, f_index = (lax.axis_index(a) for a in ("tile", "src", "focus"))
-    rank = s_index % group
-    i32 = jnp.int32
+
+    def group_corner(d):
+        return lax.rem(lax.axis_index("src") + d, group)
+
+    def fixed_corner(c):
+        return lambda d: c
+
     tables = {name: jnp.asarray(value) for name, value in make_tables(tile, freqs, AMBIT).items()}
     tables["right1t"] = jnp.asarray(
         np.swapaxes(np.asarray(make_tables(tile, freqs, AMBIT)["right1"]), 1, 2)
@@ -339,49 +351,52 @@
 
     got = []
     if group > 1:
-        where = jnp.stack([f_index] + [(rank + d) % group for d in range(1, group)]).astype(i32)
         sends = call(
-            lambda *refs: send_kernel(sources, *refs),
+            lambda *refs: send_kernel(sources, lambda d: group_corner(d + 1), *refs),
             Shape(group - 1, local_src, freqs, 2 * freqs),
-            [SMEM, SMEM, VMEM],
-        )(where, weights, pupil)
+            [SMEM, VMEM],
+        )(weights, pupil)
         got = [hop_group(sends[d - 1], d) for d in range(1, group)]
-    edge = call(edge_kernel, Shape(freqs, 2 * freqs), [SMEM, VMEM, VMEM, VMEM])(
-        jnp.stack([f_index]).astype(i32), mask, tables["row"], tables["edge"]
+    edge = call(edge_kernel, Shape(freqs, 2 * freqs), [VMEM, VMEM, VMEM])(
+        mask, tables["row"], tables["edge"]
     )
     near = hop_tile(edge, 0)
     spec, own_pack = call(
-        lambda *refs: own_kernel(sources, *refs),
+        lambda *refs: own_kernel(sources, group_corner, *refs),
         [(freqs, 2 * freqs), (local_src, freqs, 2 * freqs)],
-        [SMEM, SMEM, VMEM, VMEM, VMEM, VMEM],
-    )(jnp.stack([rank]).astype(i32), weights, pupil, mask, tables["row"], tables["colt"])
+        [SMEM, VMEM, VMEM, VMEM, VMEM],
+        flops=10**9,
+    )(weights, pupil, mask, tables["row"], tables["colt"])
     specs = [spec, near, hop_focus(near)]
 
     gradient = []
     for c in range(n_corner):
         if group > 1:
             packs = [own_pack] + got
-            corner = f_index * corner_dev + rank
         else:
             packs = [
                 call(
-                    lambda *refs: send_kernel(sources, *refs),
+                    lambda *refs: send_kernel(sources, fixed_corner(c), *refs),
                     Shape(1, local_src, freqs, 2 * freqs),
-                    [SMEM, SMEM, VMEM],
-                )(jnp.array([0, c], i32), weights, pupil)[0]
+                    [SMEM, VMEM],
+                )(weights, pupil)[0]
             ]
-            corner = f_index * corner_dev + c
-        active = (corner < counts[t_index]).astype(jnp.float32)[None]
+
+        def corner_of(c=c):
+            mine = group_corner(0) if group > 1 else c
+            return lax.axis_index("focus") * corner_dev + mine
+
         n_pack = len(packs)
         field = (n_pack * local_src, grid, 2 * grid)
         if n_src == group:
             gs = call(
-                lambda *refs: main_kernel(len(specs), n_pack, *refs),
+                lambda *refs: main_kernel(len(specs), n_pack, corner_of, *refs),
                 Shape(freqs, 2 * freqs),
                 [SMEM] + [VMEM] * (len(specs) + n_pack + 7),
                 [pltpu.VMEM(field, jnp.float32)],
+                limit=24,
             )(
-                active,
+                counts,
                 *specs,
                 *packs,
                 target,
@@ -392,14 +407,16 @@
                 lambda *refs: forward_kernel(len(specs), n_pack, *refs),
                 [(grid, grid), field],
                 [VMEM] * (len(specs) + n_pack + 2),
+                limit=24,
             )(*specs, *packs, tables["right1"], tables["left2"])
             parts = [part] + [hop_src(part, r) for r in range(group, n_src, group)]
             gs = call(
-                lambda *refs: adjoint_kernel(len(parts), n_pack, *refs),
+                lambda *refs: adjoint_kernel(len(parts), n_pack, corner_of, *refs),
                 Shape(freqs, 2 * freqs),
                 [SMEM] + [VMEM] * (len(parts) + n_pack + 6),
+                limit=24,
             )(
-                active,
+                counts,
                 *parts,
                 *packs,
                 target,
@@ -409,23 +426,15 @@
         gradient.append(gs)
     gs = sum(gradient[1:]) + gradient[0] if len(gradient) > 1 else gradient[0]
     gs = gs + hop_focus(gs)
-    own = [gs] + [hop_src(gs, d) for d in range(1, n_src)]
-    near = [hop_tile(gs, d) for d in range(n_src)]
-    received = sum(near[1:]) + near[0] if len(near) > 1 else near[0]
+    gs = sum([hop_src(gs, d) for d in range(1, n_src)], gs)
+    received = hop_tile(gs, 0)
     across = hop_focus(received)
     rows = tile // (n_src * n_focus)
-    where = jnp.stack([f_index, s_index * n_focus + f_index]).astype(i32)
     return call(
-        lambda *refs: final_kernel(len(own), 1, *refs),
+        lambda *refs: final_kernel(1, 1, *refs),
         Shape(rows, tile),
-        [SMEM] + [VMEM] * (len(own) + 5),
-    )(
-        where,
-        *own,
-        received,
-        across,
-        *(tables[k] for k in ("rowt", "colown", "coledge")),
-    )
+        [VMEM] * 6,
+    )(gs, received, across, *(tables[k] for k in ("rowt", "colown", "coledge")))
 
 
 def solution(mesh):

time: 44.5 us -> 36.2 us (0.81)
  Pallas kernels: 18.6 us -> 11 us
  starting transfers between devices: 13.2 us -> 8.81 us
  waiting for transfers between devices: 7.03 us -> 11.4 us
  local copies, waits for them, and re-layouts: 2.57 us -> 4.51 us
  other arithmetic: 1.92 us -> 0.01 us
  between operations: 0.75 us -> 0.2 us
    pallas_call x5, Pallas kernels: 18.6 us -> 11 us  [the longest x1 7.48 us: per_device(): call(lambda *refs: main_kernel(len(specs), n_pack, corner_of, *refs), Sha...]
    ppermute x1, waiting for transfers between devices: 0.01 us -> 3.75 us  [hop_src(): lax.ppermute(value, 'src', [(i, (i + by) % n_src) for i in range(n_src)])]
    ppermute x3 -> x2, starting transfers between devices: 7.98 us -> 5.05 us  [hop_tile(): return lax.ppermute(value, ('tile', 'src', 'focus'), pairs)]
    unnamed x16 -> x36, local copies, waits for them, and re-layouts: 1.99 us -> 4.51 us
    ppermute x1, starting transfers between devices: 1.73 us -> 0.17 us  [hop_src(): lax.ppermute(value, 'src', [(i, (i + by) % n_src) for i in range(n_src)])]
    another operation x2 -> x0, other arithmetic: 1.15 us -> none  [the longest x1 0.6 us: per_device(): where = jnp.stack([f_index, s_index * n_focus + f_index]).astype(i32)]
    add x1, other arithmetic: 0.77 us -> 0.01 us  [per_device(): gs = gs + hop_focus(gs)]
    dynamic_slice x1 -> x0, local copies, waits for them, and re-layouts: 0.58 us -> none  [per_device(): active = (corner < counts[t_index]).astype(jnp.float32)[None]]
  transfers between devices with their start and end apart: 8 -> 7, of which waited for: 4 -> 5; matrix products, arithmetic and copies ran while one was open for 3% -> 0% of each run, Pallas kernels for 11% -> 4%
where the time goes in v2:
time: 36.2 us; the launch traced here: 35.9 us
  waiting for transfers between devices  11.4 us (31%)
  Pallas kernels  11 us (30%)
  starting transfers between devices  8.81 us (24%)
  local copies, waits for them, and re-layouts  4.51 us (12%)
    pallas_call x1, Pallas kernels, per_device(): call(lambda *refs: main_kernel(len(specs), n_pack, corner_of, *refs), Sha...  7.48 us
    ppermute x2, waiting for transfers between devices, hop_tile(): return lax.ppermute(value, ('tile', 'src', 'focus'), pairs)  5.52 us
    ppermute x2, starting transfers between devices, hop_tile(): return lax.ppermute(value, ('tile', 'src', 'focus'), pairs)  5.05 us
    unnamed x36, local copies, waits for them, and re-layouts  4.51 us
    ppermute x1, waiting for transfers between devices, hop_src(): lax.ppermute(value, 'src', [(i, (i + by) % n_src) for i in range(n_src)])  3.75 us
    ppermute x1, starting transfers between devices, hop_group(): return lax.ppermute(value, 'src', pairs)  3.03 us
    ppermute x3, waiting for transfers between devices, hop_focus(): return lax.ppermute(value, 'focus', [(0, 1), (1, 0)])  2.09 us
    pallas_call x1, Pallas kernels, per_device(): call(lambda *refs: final_kernel(1, 1, *refs), Shape(rows, tile), [VMEM] * 6)  1.25 us
  transfers between devices with their start and end apart: 7, of which 5 were waited for; matrix products, arithmetic and copies ran while one was open for 0% of the time, Pallas kernels for 4%

profile of v2, /device:TPU:0, one launch (start us, length us, event | category | flops | bytes accessed | tf_op | source)
XLA Modules:
  0.0 35.9 jit_solution(14580692861142734605)
XLA Ops:
  0.0 1.2 %copy-done = f32[2,8,2,64,64]{4,3,2,1,0:T(8,128)S(1)} copy-done((f32[2,8,2,64,64]{4,3,2,1,0:T(8,128)S(1)}, f32[2,8,2,64,64]{4,3,2,1,0:T(8,128)}, u32[]{:S(2)}) %copy-start) | copy-done | bytes 524312
  1.2 0.7 %copy-done.15 = f32[8]{0:T(128)S(1)} copy-done((f32[8]{0:T(128)S(1)}, f32[8]{0:T(128)}, u32[]{:S(2)}) %copy-start.15) | copy-done | bytes 56
  1.9 0.7 %shard_map.165 = f32[1,8,64,128]{3,2,1,0:T(8,128)S(1)} custom-call(f32[8]{0:T(128)S(1)} %copy-done.15, f32[2,8,2,64,64]{4,3,2,1,0:T(8,128)S(1)} %copy-done), custom_call_target="tpu_custom_call" | custom-call | bytes 1048576 | tf_op jit(solution)/shard_map/pallas_call | solution.py:354
  2.6 3.0 %collective-permute-start.2 = (f32[8,64,128]{2,1,0:T(8,128)S(1)}, f32[8,64,128]{2,1,0:T(8,128)S(1)}, u32[]{:S(2)}, u32[]{:S(2)}) collective-permute-start(f32[8,64,128]{2,1,0:T(8,128)S(1)} %bitcast.1), channel_id=1, source_target_pairs={{0,2},{2,0},{1,3},{3,1},{4,6},{6,4},{5,7},{7,5},{8,10},{10,8},{9,1... | collective-permute-start | bytes 786440 | tf_op jit(solution)/shard_map/ppermute | solution.py:335
  5.6 1.1 %copy-done.4 = f32[384,384]{1,0:T(8,128)S(1)} copy-done((f32[384,384]{1,0:T(8,128)S(1)}, f32[384,384]{1,0:T(8,128)}, u32[]{:S(2)}) %copy-start.4) | copy-done | bytes 589848
  6.7 0.9 %copy-done.14 = bf16[2,2,128,128]{3,2,1,0:T(8,128)(2,1)S(1)} copy-done((bf16[2,2,128,128]{3,2,1,0:T(8,128)(2,1)S(1)}, bf16[2,2,128,128]{3,2,1,0:T(8,128)(2,1)}, u32[]{:S(2)}) %copy-start.14) | copy-done | bytes 131096
  7.6 0.5 %shard_map.164 = f32[64,128]{1,0:T(8,128)S(1)} custom-call(f32[384,384]{1,0:T(8,128)S(1)} %copy-done.4, bf16[2,128,384]{2,1,0:T(8,128)(2,1)S(1)} %copy-done.2, bf16[2,2,128,128]{3,2,1,0:T(8,128)(2,1)S(1)} %copy-done.14), custom_call_target="tpu_custom_call" | custom-call | bytes 1048576 | tf_op jit(solution)/shard_map/pallas_call | solution.py:360
  8.1 0.0 copy-start.6
  8.1 0.0 copy-start.7
  8.1 0.0 copy-start.9
  8.1 2.8 %collective-permute-start = (f32[64,128]{1,0:T(8,128)S(1)}, f32[64,128]{1,0:T(8,128)S(1)}, u32[]{:S(2)}, u32[]{:S(2)}) collective-permute-start(f32[64,128]{1,0:T(8,128)S(1)} %shard_map.164), channel_id=1, source_target_pairs={{0,5},{5,0},{2,7},{7,2},{4,9},{9,4},{6,11},{11,6},{8,13},{13,8},{1... | collective-permute-start | bytes 98312 | tf_op jit(solution)/shard_map/ppermute | solution.py:350
  10.9 2.6 %collective-permute-done.refs_2_ = f32[64,128]{1,0:T(8,128)S(1)} collective-permute-done((f32[64,128]{1,0:T(8,128)S(1)}, f32[64,128]{1,0:T(8,128)S(1)}, u32[]{:S(2)}, u32[]{:S(2)}) %collective-permute-start) | collective-permute-done | bytes 32800 | tf_op jit(solution)/shard_map/ppermute | solution.py:350
  13.5 1.1 %shard_map.163 = (f32[64,128]{1,0:T(8,128)S(1)}, f32[8,64,128]{2,1,0:T(8,128)S(1)}) custom-call(f32[8]{0:T(128)S(1)} %copy-done.16, f32[2,8,2,64,64]{4,3,2,1,0:T(8,128)S(1)} %copy-done.1, f32[384,384]{1,0:T(8,128)S(1)} %copy-done.5, bf16[2,128,384]{2,1,0:T(8,128)(2,1)S(1)} %copy-done.2, bf16[2,384,128]{2,1,0:T(8,128)(2,1)S(1)} %copy-done.8), custom_call_target="tpu_custom_call" | custom-call | flops 1000000000 | bytes 1048576 | tf_op jit(solution)/shard_map/pallas_call | solution.py:364
  14.7 0.0 collective-permute-done.1.refs_3_
  14.8 0.6 %copy-done.17 = s32[4]{0:T(128)S(1)} copy-done((s32[4]{0:T(128)S(1)}, s32[4]{0:T(128)}, u32[]{:S(2)}) %copy-start.17) | copy-done | bytes 40
  15.4 7.5 %shard_map.166 = f32[64,128]{1,0:T(8,128)S(1)} custom-call(s32[4]{0:T(128)S(1)} %copy-done.17, f32[64,128]{1,0:T(8,128)S(1)} %get-tuple-element.7.refs_1_, f32[64,128]{1,0:T(8,128)S(1)} %collective-permute-done.refs_2_, f32[64,128]{1,0:T(8,128)S(1)} %collective-permute-done.1.refs_3_, f32[8,64,128]{2,1,0:T(8,128)S(1)} %get-tuple-element.8.refs_4_, ...), custom_call_target="tpu_custom_call" | custom-call | bytes 1048576 | tf_op jit(solution)/shard_map/pallas_call | solution.py:392
  22.9 0.6 %collective-permute-start.3 = (f32[64,128]{1,0:T(8,128)S(1)}, f32[64,128]{1,0:T(8,128)S(1)}, u32[]{:S(2)}, u32[]{:S(2)}) collective-permute-start(f32[64,128]{1,0:T(8,128)S(1)} %shard_map.166), channel_id=1, source_target_pairs={{0,1},{1,0},{2,3},{3,2},{4,5},{5,4},{6,7},{7,6},{8,9},{9,8},{10,11... | collective-permute-start | bytes 98312 | tf_op jit(solution)/shard_map/ppermute | solution.py:338
  23.4 0.9 %collective-permute-done.3 = f32[64,128]{1,0:T(8,128)S(1)} collective-permute-done((f32[64,128]{1,0:T(8,128)S(1)}, f32[64,128]{1,0:T(8,128)S(1)}, u32[]{:S(2)}, u32[]{:S(2)}) %collective-permute-start.3) | collective-permute-done | bytes 32800 | tf_op jit(solution)/shard_map/ppermute | solution.py:338
  24.3 0.2 collective-permute-start.4
  24.4 3.7 %collective-permute-done.4 = f32[64,128]{1,0:T(8,128)S(1)} collective-permute-done((f32[64,128]{1,0:T(8,128)S(1)}, f32[64,128]{1,0:T(8,128)S(1)}, u32[]{:S(2)}, u32[]{:S(2)}) %collective-permute-start.4) | collective-permute-done | bytes 32800 | tf_op jit(solution)/shard_map/ppermute | solution.py:331
  28.2 2.3 %collective-permute-start.5 = (f32[64,128]{1,0:T(8,128)S(1)}, f32[64,128]{1,0:T(8,128)S(1)}, u32[]{:S(2)}, u32[]{:S(2)}) collective-permute-start(f32[64,128]{1,0:T(8,128)S(1)} %add.7.refs_0_), channel_id=1, source_target_pairs={{0,5},{5,0},{2,7},{7,2},{4,9},{9,4},{6,11},{11,6},{8,13},{13,8},{1... | collective-permute-start | bytes 98312 | tf_op jit(solution)/shard_map/ppermute | solution.py:350
  30.5 2.9 %collective-permute-done.5.refs_1_ = f32[64,128]{1,0:T(8,128)S(1)} collective-permute-done((f32[64,128]{1,0:T(8,128)S(1)}, f32[64,128]{1,0:T(8,128)S(1)}, u32[]{:S(2)}, u32[]{:S(2)}) %collective-permute-start.5) | collective-permute-done | bytes 32800 | tf_op jit(solution)/shard_map/ppermute | solution.py:350
  33.4 1.2 %collective-permute-done.6.refs_2_ = f32[64,128]{1,0:T(8,128)S(1)} collective-permute-done((f32[64,128]{1,0:T(8,128)S(1)}, f32[64,128]{1,0:T(8,128)S(1)}, u32[]{:S(2)}, u32[]{:S(2)}) %collective-permute-start.6) | collective-permute-done | bytes 32800 | tf_op jit(solution)/shard_map/ppermute | solution.py:338
  34.6 1.2 %shard_map.167 = f32[96,384]{1,0:T(8,128)} custom-call(f32[64,128]{1,0:T(8,128)S(1)} %add.7.refs_0_, f32[64,128]{1,0:T(8,128)S(1)} %collective-permute-done.5.refs_1_, f32[64,128]{1,0:T(8,128)S(1)} %collective-permute-done.6.refs_2_, bf16[2,384,128]{2,1,0:T(8,128)(2,1)S(1)} %copy-done.8, bf16[2,128,384]{2,1,0:T(8,128)(2,1)S(1)} %copy-done.2, ...), custom_call_target="tpu_custom_call" | custom-call | bytes 1048576 | tf_op jit(solution)/shard_map/pallas_call | solution.py:433
  (33 shorter events, 0.1 us)
Async XLA Ops:
  0.0 1.2 %copy-start = (f32[2,8,2,64,64]{4,3,2,1,0:T(8,128)S(1)}, f32[2,8,2,64,64]{4,3,2,1,0:T(8,128)}, u32[]{:S(2)}) copy-start(f32[2,8,2,64,64]{4,3,2,1,0:T(8,128)} %refs_1_.3) | copy-start | bytes 1572868
  1.9 3.7 %copy-start.2 = (bf16[2,128,384]{2,1,0:T(8,128)(2,1)S(1)}, bf16[2,128,384]{2,1,0:T(8,128)(2,1)}, u32[]{:S(2)}) copy-start(bf16[2,128,384]{2,1,0:T(8,128)(2,1)} %constant.20.clone.refs_3_.row_ref.refs_4_) | copy-start | bytes 589828
  1.9 11.6 %copy-start.1 = (f32[2,8,2,64,64]{4,3,2,1,0:T(8,128)S(1)}, f32[2,8,2,64,64]{4,3,2,1,0:T(8,128)}, u32[]{:S(2)}) copy-start(f32[2,8,2,64,64]{4,3,2,1,0:T(8,128)} %refs_1_.3) | copy-start | bytes 1572868
  2.6 12.1 %collective-permute-start.2 = (f32[8,64,128]{2,1,0:T(8,128)S(1)}, f32[8,64,128]{2,1,0:T(8,128)S(1)}, u32[]{:S(2)}, u32[]{:S(2)}) collective-permute-start(f32[8,64,128]{2,1,0:T(8,128)S(1)} %bitcast.1), channel_id=1, source_target_pairs={{0,2},{2,0},{1,3},{3,1},{4,6},{6,4},{5,7},{7,5},{8,10},{10,8},{9,1... | collective-permute-start | bytes 786440 | tf_op jit(solution)/shard_map/ppermute | solution.py:335
  5.6 1.1 %copy-start.4 = (f32[384,384]{1,0:T(8,128)S(1)}, f32[384,384]{1,0:T(8,128)}, u32[]{:S(2)}) copy-start(f32[384,384]{1,0:T(8,128)} %mask_ref.1) | copy-start | bytes 1769476
  6.7 0.9 %copy-start.14 = (bf16[2,2,128,128]{3,2,1,0:T(8,128)(2,1)S(1)}, bf16[2,2,128,128]{3,2,1,0:T(8,128)(2,1)}, u32[]{:S(2)}) copy-start(bf16[2,2,128,128]{3,2,1,0:T(8,128)(2,1)} %constant.22.clone.edge_ref) | copy-start | bytes 393220
  7.6 5.9 %copy-start.5 = (f32[384,384]{1,0:T(8,128)S(1)}, f32[384,384]{1,0:T(8,128)}, u32[]{:S(2)}) copy-start(f32[384,384]{1,0:T(8,128)} %mask_ref.1) | copy-start | bytes 1769476
  7.6 5.9 %copy-start.8 = (bf16[2,384,128]{2,1,0:T(8,128)(2,1)S(1)}, bf16[2,384,128]{2,1,0:T(8,128)(2,1)}, u32[]{:S(2)}) copy-start(bf16[2,384,128]{2,1,0:T(8,128)(2,1)} %constant.21.clone.refs_4_.refs_3_) | copy-start | bytes 589828
  7.6 5.9 %copy-start.16 = (f32[8]{0:T(128)S(1)}, f32[8]{0:T(128)}, u32[]{:S(2)}) copy-start(f32[8]{0:T(128)} %refs_0_.4) | copy-start | bytes 100
  8.0 6.7 %copy-start.3 = (f32[384,384]{1,0:T(8,128)S(1)}, f32[384,384]{1,0:T(8,128)}, u32[]{:S(2)}) copy-start(f32[384,384]{1,0:T(8,128)} %refs_6_.1) | copy-start | bytes 1769476
  8.1 6.7 %copy-start.6 = (bf16[2,128,384]{2,1,0:T(8,128)(2,1)S(1)}, bf16[2,128,384]{2,1,0:T(8,128)(2,1)}, u32[]{:S(2)}) copy-start(bf16[2,128,384]{2,1,0:T(8,128)(2,1)} %constant.27.clone.refs_12_) | copy-start | bytes 589828
  8.1 6.7 %copy-start.7 = (bf16[2,384,128]{2,1,0:T(8,128)(2,1)S(1)}, bf16[2,384,128]{2,1,0:T(8,128)(2,1)}, u32[]{:S(2)}) copy-start(bf16[2,384,128]{2,1,0:T(8,128)(2,1)} %constant.26.clone.refs_11_) | copy-start | bytes 589828
  8.1 6.7 %copy-start.9 = (bf16[2,256,128]{2,1,0:T(8,128)(2,1)S(1)}, bf16[2,256,128]{2,1,0:T(8,128)(2,1)}, u32[]{:S(2)}) copy-start(bf16[2,256,128]{2,1,0:T(8,128)(2,1)} %constant.29.clone.refs_8_) | copy-start | bytes 393220
  8.1 6.7 %copy-start.10 = (bf16[256,256]{1,0:T(8,128)(2,1)S(1)}, bf16[256,256]{1,0:T(8,128)(2,1)}, u32[]{:S(2)}) copy-start(bf16[256,256]{1,0:T(8,128)(2,1)} %constant.25.clone.refs_10_) | copy-start | bytes 393220
  8.1 6.7 %copy-start.11 = (bf16[256,192]{1,0:T(8,128)(2,1)S(1)}, bf16[256,192]{1,0:T(8,128)(2,1)}, u32[]{:S(2)}) copy-start(bf16[256,192]{1,0:T(8,128)(2,1)} %constant.24.clone.refs_9_) | copy-start | bytes 294916
  8.1 6.7 %copy-start.12 = (bf16[2,128,256]{2,1,0:T(8,128)(2,1)S(1)}, bf16[2,128,256]{2,1,0:T(8,128)(2,1)}, u32[]{:S(2)}) copy-start(bf16[2,128,256]{2,1,0:T(8,128)(2,1)} %constant.23.clone.refs_7_) | copy-start | bytes 393220
  8.1 5.4 %collective-permute-start = (f32[64,128]{1,0:T(8,128)S(1)}, f32[64,128]{1,0:T(8,128)S(1)}, u32[]{:S(2)}, u32[]{:S(2)}) collective-permute-start(f32[64,128]{1,0:T(8,128)S(1)} %shard_map.164), channel_id=1, source_target_pairs={{0,5},{5,0},{2,7},{7,2},{4,9},{9,4},{6,11},{11,6},{8,13},{13,8},{1... | collective-permute-start | bytes 98312 | tf_op jit(solution)/shard_map/ppermute | solution.py:350
  13.5 1.2 %collective-permute-start.1 = (f32[64,128]{1,0:T(8,128)S(1)}, f32[64,128]{1,0:T(8,128)S(1)}, u32[]{:S(2)}, u32[]{:S(2)}) collective-permute-start(f32[64,128]{1,0:T(8,128)S(1)} %collective-permute-done.refs_2_), channel_id=1, source_target_pairs={{0,1},{1,0},{2,3},{3,2},{4,5},{5,4},{6,7},{7,6},{8,9},{9,8},{10,11... | collective-permute-start | bytes 98312 | tf_op jit(solution)/shard_map/ppermute | solution.py:338
  14.7 0.7 %copy-start.17 = (s32[4]{0:T(128)S(1)}, s32[4]{0:T(128)}, u32[]{:S(2)}) copy-start(s32[4]{0:T(128)} %refs_0_.5) | copy-start | bytes 52
  22.9 11.8 %copy-start.13 = (bf16[2,2,128,128]{3,2,1,0:T(8,128)(2,1)S(1)}, bf16[2,2,128,128]{3,2,1,0:T(8,128)(2,1)}, u32[]{:S(2)}) copy-start(bf16[2,2,128,128]{3,2,1,0:T(8,128)(2,1)} %constant.28.clone.refs_5_) | copy-start | bytes 393220
  22.9 1.4 %collective-permute-start.3 = (f32[64,128]{1,0:T(8,128)S(1)}, f32[64,128]{1,0:T(8,128)S(1)}, u32[]{:S(2)}, u32[]{:S(2)}) collective-permute-start(f32[64,128]{1,0:T(8,128)S(1)} %shard_map.166), channel_id=1, source_target_pairs={{0,1},{1,0},{2,3},{3,2},{4,5},{5,4},{6,7},{7,6},{8,9},{9,8},{10,11... | collective-permute-start | bytes 98312 | tf_op jit(solution)/shard_map/ppermute | solution.py:338
  24.3 3.9 %collective-permute-start.4 = (f32[64,128]{1,0:T(8,128)S(1)}, f32[64,128]{1,0:T(8,128)S(1)}, u32[]{:S(2)}, u32[]{:S(2)}) collective-permute-start(f32[64,128]{1,0:T(8,128)S(1)} %add.6), channel_id=1, source_target_pairs={{0,2},{2,0},{1,3},{3,1},{4,6},{6,4},{5,7},{7,5},{8,10},{10,8},{9,1... | collective-permute-start | bytes 98312 | tf_op jit(solution)/shard_map/ppermute | solution.py:331
  28.2 5.2 %collective-permute-start.5 = (f32[64,128]{1,0:T(8,128)S(1)}, f32[64,128]{1,0:T(8,128)S(1)}, u32[]{:S(2)}, u32[]{:S(2)}) collective-permute-start(f32[64,128]{1,0:T(8,128)S(1)} %add.7.refs_0_), channel_id=1, source_target_pairs={{0,5},{5,0},{2,7},{7,2},{4,9},{9,4},{6,11},{11,6},{8,13},{13,8},{1... | collective-permute-start | bytes 98312 | tf_op jit(solution)/shard_map/ppermute | solution.py:350
  33.4 1.2 %collective-permute-start.6 = (f32[64,128]{1,0:T(8,128)S(1)}, f32[64,128]{1,0:T(8,128)S(1)}, u32[]{:S(2)}, u32[]{:S(2)}) collective-permute-start(f32[64,128]{1,0:T(8,128)S(1)} %collective-permute-done.5.refs_1_), channel_id=1, source_target_pairs={{0,1},{1,0},{2,3},{3,2},{4,5},{5,4},{6,7},{7,6},{8,9},{9,8},{10,11... | collective-permute-start | bytes 98312 | tf_op jit(solution)/shard_map/ppermute | solution.py:338
  (1 other events, 0.7 us)

commit v3 on v2

--- a/solution.py
+++ b/solution.py
@@ -12,6 +12,8 @@
 
 RESIST_SLOPE = 4.0
 RESIST_LEVEL = 0.5
+
+BATCH = 4
 
 VMEM = pl.BlockSpec(memory_space=pltpu.VMEM)
 SMEM = pl.BlockSpec(memory_space=pltpu.SMEM)
@@ -143,54 +145,124 @@
         pack_ref[s] = pack(pupil_ref, s, corner_of(0), scale)
 
 
-def forward(spec, pupil_of, count, right1_ref, left2_ref, field_ref):
-    freqs, grid = spec.shape[0], right1_ref.shape[2] // 2
+def fold(z, sign):
+    half = z.shape[0] // 2
+    return z[:half] + swapped_halves(z[half:]) * sign
+
+
+def lane_sign(freqs):
+    return jnp.where(left_lanes((1, 2 * freqs)), -1.0, 1.0)
+
+
+def forward(spec, pupil_of, pairs, right1, left2_ref, field_ref, data_ref, rows_ref):
+    freqs, lanes = spec.shape
+    grid = lanes
     turned = swapped_halves(spec)
     low = left_lanes(spec.shape)
     spec_a = jnp.where(low, spec, turned)
     spec_b = jnp.where(low, -turned, spec)
-    right1 = (right1_ref[0], right1_ref[1])
+    sign = lane_sign(freqs)
     left2 = left2_ref[...]
-    total = jnp.zeros((grid, grid), jnp.float32)
-    for s in range(count):
-        p = pupil_of(s)
-        g = p * spec_a + swapped_halves(p) * spec_b
-        hh, hl = split(mm3(split(g), right1))
-        f = mm(left2, jnp.concatenate([hh, hl, hh], axis=0))
-        e_re = f[:grid, :grid] - f[grid:, grid:]
-        e_im = f[:grid, grid:] + f[grid:, :grid]
-        field_ref[s, :, :grid] = e_re
-        field_ref[s, :, grid:] = e_im
-        total = total + (e_re * e_re + e_im * e_im)
-    return total
-
-
-def adjoint(intensity, target, active, pupil_of, count, right1t, back2_ref, up, upt, field_ref):
+    batch = math.gcd(BATCH, pairs)
+
+    def left_product(group):
+        for j in range(batch):
+            pair = group * batch + j
+            high, low = [], []
+            for half in range(2):
+                p = pupil_of(pair, half)
+                gh, gl = split(p * spec_a + swapped_halves(p) * spec_b)
+                high.append(gh)
+                low.append(gl)
+            gh, gl = jnp.concatenate(high, axis=1), jnp.concatenate(low, axis=1)
+            f = mm(left2, jnp.concatenate([gh, gl, gh], axis=0))
+            for half in range(2):
+                hh, hl = split(fold(f[:, half * lanes : (half + 1) * lanes], sign))
+                rows_ref[2 * pair + half, :, :lanes] = hh
+                rows_ref[2 * pair + half, :, lanes : 2 * lanes] = hl
+
+    def right_product(group, total):
+        size = 2 * batch
+        rows = rows_ref[pl.ds(group * size, size), :, : 2 * lanes]
+        rows = rows.reshape(size * grid, 2 * lanes)
+        right = jnp.concatenate([right1[0][...], right1[0][...], right1[1][...]], axis=0)
+        e = mm(jnp.concatenate([rows, rows[:, :lanes]], axis=1), right)
+        for s in range(size):
+            part = e[s * grid : (s + 1) * grid]
+            field_ref[group * size + s] = part
+            part = part * part
+            total = total + (part[:, :grid] + part[:, grid:])
+        return total
+
+    def step(group, total):
+        left_product(group + 1)
+        return right_product(group, total)
+
+    groups = pairs // batch
+    left_product(0)
+    total = lax.fori_loop(0, groups - 1, step, jnp.zeros((grid, grid), jnp.float32))
+    return right_product(groups - 1, total)
+
+
+def adjoint(
+    intensity, target, active, pupil_of, pairs, right1t, back2_ref, up, upt, field_ref, data_ref, rows_ref
+):
     grid = intensity.shape[0]
-    freqs = grid // 2
-    image = mm3(up, split(mm3(split(intensity), upt)))
-    resist = jax.nn.sigmoid(RESIST_SLOPE * (image - RESIST_LEVEL))
-    slope = 2.0 * (resist - target) * RESIST_SLOPE * resist * (1.0 - resist)
-    down = mm3(split(mm3(upt, split(slope))), up) * (2.0 * active)
+    freqs, lanes = grid // 2, grid
+    up = (up[0][...], up[1][...])
+    upt = (upt[0][...], upt[1][...])
+    image = mm3(up, split(mm3(split(intensity * RESIST_SLOPE), upt)))
+    resist = jax.nn.sigmoid(image - RESIST_SLOPE * RESIST_LEVEL)
+    slope = (resist - target) * (resist * (1.0 - resist))
+    down = mm3(upt, split(mm3(split(slope), up))) * (4.0 * RESIST_SLOPE * active)
     down2 = jnp.concatenate([down, down], axis=1)
     back2 = back2_ref[...]
-    th, tl = right1t
-    both = jnp.concatenate([th, tl], axis=1)
-    t1 = jnp.zeros((freqs, 2 * freqs), jnp.float32)
-    t2 = jnp.zeros((freqs, 2 * freqs), jnp.float32)
-    for s in range(count):
-        eh, el = split(down2 * field_ref[s])
-        f = mm(back2, jnp.concatenate([eh, el], axis=0))
-        f = f[: 2 * freqs] + f[2 * freqs :]
-        h = jnp.concatenate(
-            [f[:freqs, :grid] + f[freqs:, grid:], f[:freqs, grid:] - f[freqs:, :grid]], axis=1
+    sign = -lane_sign(freqs)
+    batch = math.gcd(BATCH, pairs)
+    size = 2 * batch
+
+    def right_product(group):
+        high, low = [], []
+        for j in range(size):
+            eh, el = split(down2 * field_ref[group * size + j])
+            high.append(eh)
+            low.append(el)
+        rows = jnp.concatenate(
+            [jnp.concatenate(high, axis=0), jnp.concatenate(low, axis=0)], axis=1
         )
-        hh, hl = split(h)
-        q = mm(hh, both)
-        q = q[:, : 2 * freqs] + q[:, 2 * freqs :] + mm(hl, th)
-        p = pupil_of(s)
-        t1 = t1 + p * q
-        t2 = t2 + swapped_halves(p) * q
+        both = jnp.concatenate([right1t[0][...], right1t[1][...]], axis=1)
+        t = mm(rows, jnp.concatenate([both, both], axis=0))
+        t = t[:, :lanes] + t[:, lanes:]
+        for j in range(batch):
+            for half in range(2):
+                k = 2 * j + half
+                hh, hl = split(t[k * grid : (k + 1) * grid])
+                at = half * lanes
+                data_ref[group * batch + j, :grid, at : at + lanes] = hh
+                data_ref[group * batch + j, grid:, at : at + lanes] = hl
+
+    def left_product(group, carry):
+        t1, t2 = carry
+        for j in range(batch):
+            pair = group * batch + j
+            f = mm(back2, data_ref[pair])
+            f = f[: 2 * freqs] + f[2 * freqs :]
+            for half in range(2):
+                q = fold(f[:, half * lanes : (half + 1) * lanes], sign)
+                p = pupil_of(pair, half)
+                t1 = t1 + p * q
+                t2 = t2 + swapped_halves(p) * q
+        return t1, t2
+
+    def step(group, carry):
+        right_product(group + 1)
+        return left_product(group, carry)
+
+    groups = pairs // batch
+    zero = jnp.zeros((freqs, lanes), jnp.float32)
+    right_product(0)
+    carry = lax.fori_loop(0, groups - 1, step, (zero, zero))
+    t1, t2 = left_product(groups - 1, carry)
     low = left_lanes(t1.shape)
     return jnp.where(low, t1 + swapped_halves(t1), t2 - swapped_halves(t2))
 
@@ -201,57 +273,68 @@
 
 
 def pick(packs):
-    local = packs[0].shape[0]
-    return lambda s: packs[s // local][s % local]
+    if len(packs) == 1:
+        return lambda pair, half: packs[0][2 * pair + half]
+    return lambda pair, half: packs[half][pair]
 
 
 def main_kernel(n_spec, n_pack, corner_of, counts_ref, *refs):
     specs, refs = refs[:n_spec], refs[n_spec:]
     packs, refs = refs[:n_pack], refs[n_pack:]
-    target_ref, right1_ref, right1t_ref, left2_ref, back2_ref, up_ref, upt_ref = refs[:7]
-    out_ref, field_ref = refs[7:]
+    target_ref, right1_ref, left2_ref, right1t_ref, back2_ref, up_ref, upt_ref = refs[:7]
+    out_ref, field_ref, data_ref, rows_ref = refs[7:]
     spec = sum(ref[...] for ref in specs[1:]) + specs[0][...]
     pupil_of = pick(packs)
-    count = n_pack * packs[0].shape[0]
-    intensity = forward(spec, pupil_of, count, right1_ref, left2_ref, field_ref)
+    count = n_pack * packs[0].shape[0] // 2
+    work = (field_ref, data_ref, rows_ref)
+    intensity = forward(spec, pupil_of, count, pair_of(right1_ref), left2_ref, *work)
     out_ref[...] = adjoint(
         intensity,
         target_ref[...],
         active_here(corner_of, counts_ref),
         pupil_of,
         count,
-        (right1t_ref[0], right1t_ref[1]),
+        pair_of(right1t_ref),
         back2_ref,
-        (up_ref[0], up_ref[1]),
-        (upt_ref[0], upt_ref[1]),
-        field_ref,
-    )
+        pair_of(up_ref),
+        pair_of(upt_ref),
+        *work,
+    )
+
+
+def pair_of(ref):
+    return ref.at[0], ref.at[1]
 
 
 def forward_kernel(n_spec, n_pack, *refs):
     specs, refs = refs[:n_spec], refs[n_spec:]
     packs, refs = refs[:n_pack], refs[n_pack:]
-    right1_ref, left2_ref, intensity_ref, field_ref = refs
+    right1_ref, left2_ref, intensity_ref, field_ref, data_ref, rows_ref = refs
     spec = sum(ref[...] for ref in specs[1:]) + specs[0][...]
-    count = n_pack * packs[0].shape[0]
-    intensity_ref[...] = forward(spec, pick(packs), count, right1_ref, left2_ref, field_ref)
+    count = n_pack * packs[0].shape[0] // 2
+    intensity_ref[...] = forward(
+        spec, pick(packs), count, pair_of(right1_ref), left2_ref, field_ref, data_ref, rows_ref
+    )
 
 
 def adjoint_kernel(n_part, n_pack, corner_of, counts_ref, *refs):
     parts, refs = refs[:n_part], refs[n_part:]
     packs, refs = refs[:n_pack], refs[n_pack:]
-    target_ref, right1t_ref, back2_ref, up_ref, upt_ref, field_ref, out_ref = refs
+    target_ref, right1t_ref, back2_ref, up_ref, upt_ref, field_ref = refs[:6]
+    out_ref, data_ref, rows_ref = refs[6:]
     out_ref[...] = adjoint(
         sum(ref[...] for ref in parts[1:]) + parts[0][...],
         target_ref[...],
         active_here(corner_of, counts_ref),
         pick(packs),
-        n_pack * packs[0].shape[0],
-        (right1t_ref[0], right1t_ref[1]),
+        n_pack * packs[0].shape[0] // 2,
+        pair_of(right1t_ref),
         back2_ref,
-        (up_ref[0], up_ref[1]),
-        (upt_ref[0], upt_ref[1]),
+        pair_of(up_ref),
+        pair_of(upt_ref),
         field_ref,
+        data_ref,
+        rows_ref,
     )
 
 
@@ -386,43 +469,40 @@
             mine = group_corner(0) if group > 1 else c
             return lax.axis_index("focus") * corner_dev + mine
 
+        if len(packs) > 2:
+            packs = [jnp.concatenate(packs)]
         n_pack = len(packs)
-        field = (n_pack * local_src, grid, 2 * grid)
+        count = n_pack * local_src
+        field = (count, grid, 2 * grid)
+        work = [
+            pltpu.VMEM((count // 2, 2 * grid, 2 * grid), jnp.bfloat16),
+            pltpu.VMEM((count, grid, 2 * grid), jnp.bfloat16),
+        ]
+        before, after = ("right1", "left2"), ("right1t", "back2", "up", "upt")
         if n_src == group:
             gs = call(
                 lambda *refs: main_kernel(len(specs), n_pack, corner_of, *refs),
                 Shape(freqs, 2 * freqs),
                 [SMEM] + [VMEM] * (len(specs) + n_pack + 7),
-                [pltpu.VMEM(field, jnp.float32)],
+                [pltpu.VMEM(field, jnp.float32)] + work,
                 limit=24,
-            )(
-                counts,
-                *specs,
-                *packs,
-                target,
-                *(tables[k] for k in ("right1", "right1t", "left2", "back2", "up", "upt")),
-            )
+            )(counts, *specs, *packs, target, *(tables[k] for k in before + after))
         else:
             part, fields = call(
                 lambda *refs: forward_kernel(len(specs), n_pack, *refs),
                 [(grid, grid), field],
                 [VMEM] * (len(specs) + n_pack + 2),
+                work,
                 limit=24,
-            )(*specs, *packs, tables["right1"], tables["left2"])
+            )(*specs, *packs, *(tables[k] for k in before))
             parts = [part] + [hop_src(part, r) for r in range(group, n_src, group)]
             gs = call(
                 lambda *refs: adjoint_kernel(len(parts), n_pack, corner_of, *refs),
                 Shape(freqs, 2 * freqs),
                 [SMEM] + [VMEM] * (len(parts) + n_pack + 6),
+                work,
                 limit=24,
-            )(
-                counts,
-                *parts,
-                *packs,
-                target,
-                *(tables[k] for k in ("right1t", "back2", "up", "upt")),
-                fields,
-            )
+            )(counts, *parts, *packs, target, *(tables[k] for k in after), fields)
         gradient.append(gs)
     gs = sum(gradient[1:]) + gradient[0] if len(gradient) > 1 else gradient[0]
     gs = gs + hop_focus(gs)

time: 36.2 us -> 33.1 us (0.914)
  Pallas kernels: 11 us -> 7.97 us
    pallas_call x1, Pallas kernels: 7.48 us -> 4.45 us  [per_device(): call(lambda *refs: main_kernel(len(specs), n_pack, corner_of, *refs), Sha...]
  transfers between devices with their start and end apart: 7 -> 7, of which waited for: 5 -> 5; matrix products, arithmetic and copies ran while one was open for 0% -> 0% of each run, Pallas kernels for 4% -> 5%
where the time goes in v3:
time: 33.1 us; the launch traced here: 32.9 us
  waiting for transfers between devices  11.4 us (34%)
  starting transfers between devices  8.81 us (27%)
  Pallas kernels  7.97 us (24%)
  local copies, waits for them, and re-layouts  4.51 us (14%)
    ppermute x2, waiting for transfers between devices, hop_tile(): return lax.ppermute(value, ('tile', 'src', 'focus'), pairs)  5.52 us
    ppermute x2, starting transfers between devices, hop_tile(): return lax.ppermute(value, ('tile', 'src', 'focus'), pairs)  5.05 us
    unnamed x36, local copies, waits for them, and re-layouts  4.51 us
    pallas_call x1, Pallas kernels, per_device(): call(lambda *refs: main_kernel(len(specs), n_pack, corner_of, *refs), Sha...  4.45 us
    ppermute x1, waiting for transfers between devices, hop_src(): lax.ppermute(value, 'src', [(i, (i + by) % n_src) for i in range(n_src)])  3.75 us
    ppermute x1, starting transfers between devices, hop_group(): return lax.ppermute(value, 'src', pairs)  3.03 us
    ppermute x3, waiting for transfers between devices, hop_focus(): return lax.ppermute(value, 'focus', [(0, 1), (1, 0)])  2.09 us
    pallas_call x1, Pallas kernels, per_device(): call(lambda *refs: final_kernel(1, 1, *refs), Shape(rows, tile), [VMEM] * 6)  1.25 us
  transfers between devices with their start and end apart: 7, of which 5 were waited for; matrix products, arithmetic and copies ran while one was open for 0% of the time, Pallas kernels for 5%

profile of v3, /device:TPU:0, one launch (start us, length us, event | category | flops | bytes accessed | tf_op | source)
XLA Modules:
  0.0 32.9 jit_solution(11849207200441447709)
XLA Ops:
  0.0 1.2 %copy-done = f32[2,8,2,64,64]{4,3,2,1,0:T(8,128)S(1)} copy-done((f32[2,8,2,64,64]{4,3,2,1,0:T(8,128)S(1)}, f32[2,8,2,64,64]{4,3,2,1,0:T(8,128)}, u32[]{:S(2)}) %copy-start) | copy-done | bytes 524312
  1.2 0.7 %copy-done.15 = f32[8]{0:T(128)S(1)} copy-done((f32[8]{0:T(128)S(1)}, f32[8]{0:T(128)}, u32[]{:S(2)}) %copy-start.15) | copy-done | bytes 56
  1.9 0.7 %shard_map.165 = f32[1,8,64,128]{3,2,1,0:T(8,128)S(1)} custom-call(f32[8]{0:T(128)S(1)} %copy-done.15, f32[2,8,2,64,64]{4,3,2,1,0:T(8,128)S(1)} %copy-done), custom_call_target="tpu_custom_call" | custom-call | bytes 1048576 | tf_op jit(solution)/shard_map/pallas_call | solution.py:437
  2.6 3.0 %collective-permute-start.2 = (f32[8,64,128]{2,1,0:T(8,128)S(1)}, f32[8,64,128]{2,1,0:T(8,128)S(1)}, u32[]{:S(2)}, u32[]{:S(2)}) collective-permute-start(f32[8,64,128]{2,1,0:T(8,128)S(1)} %bitcast.1), channel_id=1, source_target_pairs={{0,2},{2,0},{1,3},{3,1},{4,6},{6,4},{5,7},{7,5},{8,10},{10,8},{9,1... | collective-permute-start | bytes 786440 | tf_op jit(solution)/shard_map/ppermute | solution.py:418
  5.6 1.1 %copy-done.4 = f32[384,384]{1,0:T(8,128)S(1)} copy-done((f32[384,384]{1,0:T(8,128)S(1)}, f32[384,384]{1,0:T(8,128)}, u32[]{:S(2)}) %copy-start.4) | copy-done | bytes 589848
  6.7 0.9 %copy-done.14 = bf16[2,2,128,128]{3,2,1,0:T(8,128)(2,1)S(1)} copy-done((bf16[2,2,128,128]{3,2,1,0:T(8,128)(2,1)S(1)}, bf16[2,2,128,128]{3,2,1,0:T(8,128)(2,1)}, u32[]{:S(2)}) %copy-start.14) | copy-done | bytes 131096
  7.6 0.5 %shard_map.164 = f32[64,128]{1,0:T(8,128)S(1)} custom-call(f32[384,384]{1,0:T(8,128)S(1)} %copy-done.4, bf16[2,128,384]{2,1,0:T(8,128)(2,1)S(1)} %copy-done.2, bf16[2,2,128,128]{3,2,1,0:T(8,128)(2,1)S(1)} %copy-done.14), custom_call_target="tpu_custom_call" | custom-call | bytes 1048576 | tf_op jit(solution)/shard_map/pallas_call | solution.py:443
  8.1 0.0 copy-start.6
  8.1 0.0 copy-start.7
  8.1 0.0 copy-start.9
  8.1 2.8 %collective-permute-start = (f32[64,128]{1,0:T(8,128)S(1)}, f32[64,128]{1,0:T(8,128)S(1)}, u32[]{:S(2)}, u32[]{:S(2)}) collective-permute-start(f32[64,128]{1,0:T(8,128)S(1)} %shard_map.164), channel_id=1, source_target_pairs={{0,5},{5,0},{2,7},{7,2},{4,9},{9,4},{6,11},{11,6},{8,13},{13,8},{1... | collective-permute-start | bytes 98312 | tf_op jit(solution)/shard_map/ppermute | solution.py:433
  10.9 2.6 %collective-permute-done.refs_2_ = f32[64,128]{1,0:T(8,128)S(1)} collective-permute-done((f32[64,128]{1,0:T(8,128)S(1)}, f32[64,128]{1,0:T(8,128)S(1)}, u32[]{:S(2)}, u32[]{:S(2)}) %collective-permute-start) | collective-permute-done | bytes 32800 | tf_op jit(solution)/shard_map/ppermute | solution.py:433
  13.5 1.1 %shard_map.163 = (f32[64,128]{1,0:T(8,128)S(1)}, f32[8,64,128]{2,1,0:T(8,128)S(1)}) custom-call(f32[8]{0:T(128)S(1)} %copy-done.16, f32[2,8,2,64,64]{4,3,2,1,0:T(8,128)S(1)} %copy-done.1, f32[384,384]{1,0:T(8,128)S(1)} %copy-done.5, bf16[2,128,384]{2,1,0:T(8,128)(2,1)S(1)} %copy-done.2, bf16[2,384,128]{2,1,0:T(8,128)(2,1)S(1)} %copy-done.8), custom_call_target="tpu_custom_call" | custom-call | flops 1000000000 | bytes 1048576 | tf_op jit(solution)/shard_map/pallas_call | solution.py:447
  14.7 0.0 collective-permute-done.1.refs_3_
  14.8 0.6 %copy-done.17 = s32[4]{0:T(128)S(1)} copy-done((s32[4]{0:T(128)S(1)}, s32[4]{0:T(128)}, u32[]{:S(2)}) %copy-start.17) | copy-done | bytes 40
  15.4 4.4 %shard_map.166 = f32[64,128]{1,0:T(8,128)S(1)} custom-call(s32[4]{0:T(128)S(1)} %copy-done.17, f32[64,128]{1,0:T(8,128)S(1)} %get-tuple-element.7.refs_1_, f32[64,128]{1,0:T(8,128)S(1)} %collective-permute-done.refs_2_, f32[64,128]{1,0:T(8,128)S(1)} %collective-permute-done.1.refs_3_, f32[8,64,128]{2,1,0:T(8,128)S(1)} %get-tuple-element.8.refs_4_, ...), custom_call_target="tpu_custom_call" | custom-call | bytes 1048576 | tf_op jit(solution)/shard_map/pallas_call | solution.py:483
  19.8 0.5 %collective-permute-start.3 = (f32[64,128]{1,0:T(8,128)S(1)}, f32[64,128]{1,0:T(8,128)S(1)}, u32[]{:S(2)}, u32[]{:S(2)}) collective-permute-start(f32[64,128]{1,0:T(8,128)S(1)} %shard_map.166), channel_id=1, source_target_pairs={{0,1},{1,0},{2,3},{3,2},{4,5},{5,4},{6,7},{7,6},{8,9},{9,8},{10,11... | collective-permute-start | bytes 98312 | tf_op jit(solution)/shard_map/ppermute | solution.py:421
  20.4 0.9 %collective-permute-done.3 = f32[64,128]{1,0:T(8,128)S(1)} collective-permute-done((f32[64,128]{1,0:T(8,128)S(1)}, f32[64,128]{1,0:T(8,128)S(1)}, u32[]{:S(2)}, u32[]{:S(2)}) %collective-permute-start.3) | collective-permute-done | bytes 32800 | tf_op jit(solution)/shard_map/ppermute | solution.py:421
  21.3 0.2 collective-permute-start.4
  21.4 3.7 %collective-permute-done.4 = f32[64,128]{1,0:T(8,128)S(1)} collective-permute-done((f32[64,128]{1,0:T(8,128)S(1)}, f32[64,128]{1,0:T(8,128)S(1)}, u32[]{:S(2)}, u32[]{:S(2)}) %collective-permute-start.4) | collective-permute-done | bytes 32800 | tf_op jit(solution)/shard_map/ppermute | solution.py:414
  25.2 2.3 %collective-permute-start.5 = (f32[64,128]{1,0:T(8,128)S(1)}, f32[64,128]{1,0:T(8,128)S(1)}, u32[]{:S(2)}, u32[]{:S(2)}) collective-permute-start(f32[64,128]{1,0:T(8,128)S(1)} %add.7.refs_0_), channel_id=1, source_target_pairs={{0,5},{5,0},{2,7},{7,2},{4,9},{9,4},{6,11},{11,6},{8,13},{13,8},{1... | collective-permute-start | bytes 98312 | tf_op jit(solution)/shard_map/ppermute | solution.py:433
  27.5 2.9 %collective-permute-done.5.refs_1_ = f32[64,128]{1,0:T(8,128)S(1)} collective-permute-done((f32[64,128]{1,0:T(8,128)S(1)}, f32[64,128]{1,0:T(8,128)S(1)}, u32[]{:S(2)}, u32[]{:S(2)}) %collective-permute-start.5) | collective-permute-done | bytes 32800 | tf_op jit(solution)/shard_map/ppermute | solution.py:433
  30.4 1.2 %collective-permute-done.6.refs_2_ = f32[64,128]{1,0:T(8,128)S(1)} collective-permute-done((f32[64,128]{1,0:T(8,128)S(1)}, f32[64,128]{1,0:T(8,128)S(1)}, u32[]{:S(2)}, u32[]{:S(2)}) %collective-permute-start.6) | collective-permute-done | bytes 32800 | tf_op jit(solution)/shard_map/ppermute | solution.py:421
  31.6 1.2 %shard_map.167 = f32[96,384]{1,0:T(8,128)} custom-call(f32[64,128]{1,0:T(8,128)S(1)} %add.7.refs_0_, f32[64,128]{1,0:T(8,128)S(1)} %collective-permute-done.5.refs_1_, f32[64,128]{1,0:T(8,128)S(1)} %collective-permute-done.6.refs_2_, bf16[2,384,128]{2,1,0:T(8,128)(2,1)S(1)} %copy-done.8, bf16[2,128,384]{2,1,0:T(8,128)(2,1)S(1)} %copy-done.2, ...), custom_call_target="tpu_custom_call" | custom-call | bytes 1048576 | tf_op jit(solution)/shard_map/pallas_call | solution.py:513
  (33 shorter events, 0.1 us)
Async XLA Ops:
  0.0 1.2 %copy-start = (f32[2,8,2,64,64]{4,3,2,1,0:T(8,128)S(1)}, f32[2,8,2,64,64]{4,3,2,1,0:T(8,128)}, u32[]{:S(2)}) copy-start(f32[2,8,2,64,64]{4,3,2,1,0:T(8,128)} %refs_1_.3) | copy-start | bytes 1572868
  1.9 3.7 %copy-start.2 = (bf16[2,128,384]{2,1,0:T(8,128)(2,1)S(1)}, bf16[2,128,384]{2,1,0:T(8,128)(2,1)}, u32[]{:S(2)}) copy-start(bf16[2,128,384]{2,1,0:T(8,128)(2,1)} %constant.20.clone.refs_3_.row_ref.refs_4_) | copy-start | bytes 589828
  1.9 11.6 %copy-start.1 = (f32[2,8,2,64,64]{4,3,2,1,0:T(8,128)S(1)}, f32[2,8,2,64,64]{4,3,2,1,0:T(8,128)}, u32[]{:S(2)}) copy-start(f32[2,8,2,64,64]{4,3,2,1,0:T(8,128)} %refs_1_.3) | copy-start | bytes 1572868
  2.6 12.1 %collective-permute-start.2 = (f32[8,64,128]{2,1,0:T(8,128)S(1)}, f32[8,64,128]{2,1,0:T(8,128)S(1)}, u32[]{:S(2)}, u32[]{:S(2)}) collective-permute-start(f32[8,64,128]{2,1,0:T(8,128)S(1)} %bitcast.1), channel_id=1, source_target_pairs={{0,2},{2,0},{1,3},{3,1},{4,6},{6,4},{5,7},{7,5},{8,10},{10,8},{9,1... | collective-permute-start | bytes 786440 | tf_op jit(solution)/shard_map/ppermute | solution.py:418
  5.6 1.1 %copy-start.4 = (f32[384,384]{1,0:T(8,128)S(1)}, f32[384,384]{1,0:T(8,128)}, u32[]{:S(2)}) copy-start(f32[384,384]{1,0:T(8,128)} %mask_ref.1) | copy-start | bytes 1769476
  6.7 0.9 %copy-start.14 = (bf16[2,2,128,128]{3,2,1,0:T(8,128)(2,1)S(1)}, bf16[2,2,128,128]{3,2,1,0:T(8,128)(2,1)}, u32[]{:S(2)}) copy-start(bf16[2,2,128,128]{3,2,1,0:T(8,128)(2,1)} %constant.22.clone.edge_ref) | copy-start | bytes 393220
  7.6 5.9 %copy-start.5 = (f32[384,384]{1,0:T(8,128)S(1)}, f32[384,384]{1,0:T(8,128)}, u32[]{:S(2)}) copy-start(f32[384,384]{1,0:T(8,128)} %mask_ref.1) | copy-start | bytes 1769476
  7.6 5.9 %copy-start.8 = (bf16[2,384,128]{2,1,0:T(8,128)(2,1)S(1)}, bf16[2,384,128]{2,1,0:T(8,128)(2,1)}, u32[]{:S(2)}) copy-start(bf16[2,384,128]{2,1,0:T(8,128)(2,1)} %constant.21.clone.refs_4_.refs_3_) | copy-start | bytes 589828
  7.6 5.9 %copy-start.16 = (f32[8]{0:T(128)S(1)}, f32[8]{0:T(128)}, u32[]{:S(2)}) copy-start(f32[8]{0:T(128)} %refs_0_.4) | copy-start | bytes 100
  8.0 6.7 %copy-start.3 = (f32[384,384]{1,0:T(8,128)S(1)}, f32[384,384]{1,0:T(8,128)}, u32[]{:S(2)}) copy-start(f32[384,384]{1,0:T(8,128)} %refs_6_.1) | copy-start | bytes 1769476
  8.1 6.7 %copy-start.6 = (bf16[2,128,384]{2,1,0:T(8,128)(2,1)S(1)}, bf16[2,128,384]{2,1,0:T(8,128)(2,1)}, u32[]{:S(2)}) copy-start(bf16[2,128,384]{2,1,0:T(8,128)(2,1)} %constant.27.clone.refs_12_) | copy-start | bytes 589828
  8.1 6.7 %copy-start.7 = (bf16[2,384,128]{2,1,0:T(8,128)(2,1)S(1)}, bf16[2,384,128]{2,1,0:T(8,128)(2,1)}, u32[]{:S(2)}) copy-start(bf16[2,384,128]{2,1,0:T(8,128)(2,1)} %constant.26.clone.refs_11_) | copy-start | bytes 589828
  8.1 6.7 %copy-start.9 = (bf16[2,256,128]{2,1,0:T(8,128)(2,1)S(1)}, bf16[2,256,128]{2,1,0:T(8,128)(2,1)}, u32[]{:S(2)}) copy-start(bf16[2,256,128]{2,1,0:T(8,128)(2,1)} %constant.29.clone.refs_9_) | copy-start | bytes 393220
  8.1 6.7 %copy-start.10 = (bf16[256,256]{1,0:T(8,128)(2,1)S(1)}, bf16[256,256]{1,0:T(8,128)(2,1)}, u32[]{:S(2)}) copy-start(bf16[256,256]{1,0:T(8,128)(2,1)} %constant.25.clone.refs_10_) | copy-start | bytes 393220
  8.1 6.7 %copy-start.11 = (bf16[256,192]{1,0:T(8,128)(2,1)S(1)}, bf16[256,192]{1,0:T(8,128)(2,1)}, u32[]{:S(2)}) copy-start(bf16[256,192]{1,0:T(8,128)(2,1)} %constant.24.clone.refs_8_) | copy-start | bytes 294916
  8.1 6.7 %copy-start.12 = (bf16[2,128,256]{2,1,0:T(8,128)(2,1)S(1)}, bf16[2,128,256]{2,1,0:T(8,128)(2,1)}, u32[]{:S(2)}) copy-start(bf16[2,128,256]{2,1,0:T(8,128)(2,1)} %constant.23.clone.refs_7_) | copy-start | bytes 393220
  8.1 5.4 %collective-permute-start = (f32[64,128]{1,0:T(8,128)S(1)}, f32[64,128]{1,0:T(8,128)S(1)}, u32[]{:S(2)}, u32[]{:S(2)}) collective-permute-start(f32[64,128]{1,0:T(8,128)S(1)} %shard_map.164), channel_id=1, source_target_pairs={{0,5},{5,0},{2,7},{7,2},{4,9},{9,4},{6,11},{11,6},{8,13},{13,8},{1... | collective-permute-start | bytes 98312 | tf_op jit(solution)/shard_map/ppermute | solution.py:433
  13.5 1.2 %collective-permute-start.1 = (f32[64,128]{1,0:T(8,128)S(1)}, f32[64,128]{1,0:T(8,128)S(1)}, u32[]{:S(2)}, u32[]{:S(2)}) collective-permute-start(f32[64,128]{1,0:T(8,128)S(1)} %collective-permute-done.refs_2_), channel_id=1, source_target_pairs={{0,1},{1,0},{2,3},{3,2},{4,5},{5,4},{6,7},{7,6},{8,9},{9,8},{10,11... | collective-permute-start | bytes 98312 | tf_op jit(solution)/shard_map/ppermute | solution.py:421
  14.7 0.7 %copy-start.17 = (s32[4]{0:T(128)S(1)}, s32[4]{0:T(128)}, u32[]{:S(2)}) copy-start(s32[4]{0:T(128)} %refs_0_.5) | copy-start | bytes 52
  19.8 11.8 %copy-start.13 = (bf16[2,2,128,128]{3,2,1,0:T(8,128)(2,1)S(1)}, bf16[2,2,128,128]{3,2,1,0:T(8,128)(2,1)}, u32[]{:S(2)}) copy-start(bf16[2,2,128,128]{3,2,1,0:T(8,128)(2,1)} %constant.28.clone.refs_5_) | copy-start | bytes 393220
  19.8 1.4 %collective-permute-start.3 = (f32[64,128]{1,0:T(8,128)S(1)}, f32[64,128]{1,0:T(8,128)S(1)}, u32[]{:S(2)}, u32[]{:S(2)}) collective-permute-start(f32[64,128]{1,0:T(8,128)S(1)} %shard_map.166), channel_id=1, source_target_pairs={{0,1},{1,0},{2,3},{3,2},{4,5},{5,4},{6,7},{7,6},{8,9},{9,8},{10,11... | collective-permute-start | bytes 98312 | tf_op jit(solution)/shard_map/ppermute | solution.py:421
  21.3 3.9 %collective-permute-start.4 = (f32[64,128]{1,0:T(8,128)S(1)}, f32[64,128]{1,0:T(8,128)S(1)}, u32[]{:S(2)}, u32[]{:S(2)}) collective-permute-start(f32[64,128]{1,0:T(8,128)S(1)} %add.6), channel_id=1, source_target_pairs={{0,2},{2,0},{1,3},{3,1},{4,6},{6,4},{5,7},{7,5},{8,10},{10,8},{9,1... | collective-permute-start | bytes 98312 | tf_op jit(solution)/shard_map/ppermute | solution.py:414
  25.2 5.2 %collective-permute-start.5 = (f32[64,128]{1,0:T(8,128)S(1)}, f32[64,128]{1,0:T(8,128)S(1)}, u32[]{:S(2)}, u32[]{:S(2)}) collective-permute-start(f32[64,128]{1,0:T(8,128)S(1)} %add.7.refs_0_), channel_id=1, source_target_pairs={{0,5},{5,0},{2,7},{7,2},{4,9},{9,4},{6,11},{11,6},{8,13},{13,8},{1... | collective-permute-start | bytes 98312 | tf_op jit(solution)/shard_map/ppermute | solution.py:433
  30.4 1.2 %collective-permute-start.6 = (f32[64,128]{1,0:T(8,128)S(1)}, f32[64,128]{1,0:T(8,128)S(1)}, u32[]{:S(2)}, u32[]{:S(2)}) collective-permute-start(f32[64,128]{1,0:T(8,128)S(1)} %collective-permute-done.5.refs_1_), channel_id=1, source_target_pairs={{0,1},{1,0},{2,3},{3,2},{4,5},{5,4},{6,7},{7,6},{8,9},{9,8},{10,11... | collective-permute-start | bytes 98312 | tf_op jit(solution)/shard_map/ppermute | solution.py:421
  (1 other events, 0.7 us)

commit v4 on v3

--- a/solution.py
+++ b/solution.py
@@ -17,6 +17,7 @@
 
 VMEM = pl.BlockSpec(memory_space=pltpu.VMEM)
 SMEM = pl.BlockSpec(memory_space=pltpu.SMEM)
+HBM = pl.BlockSpec(memory_space=pltpu.HBM)
 
 
 def halves(value):
@@ -126,13 +127,48 @@
             out_ref[d, s] = pack(pupil_ref, s, corner_of(d), scale)
 
 
-def edge_kernel(mask_ref, row_ref, edge_ref, out_ref):
-    side = edge_ref.shape[2]
+def first_kernel(
+    sources,
+    corner_of,
+    weights_hbm,
+    pupil_hbm,
+    mask_hbm,
+    row_hbm,
+    edge_hbm,
+    edge_ref,
+    out_ref,
+    weights_ref,
+    pupil_ref,
+    mask_ref,
+    row_ref,
+    table_ref,
+    sems,
+):
+    side = edge_hbm.shape[2]
     focus = lax.axis_index("focus")
-    start = pl.multiple_of((1 - focus) * (mask_ref.shape[1] - side), 128)
-    slab = split(mask_ref[:, pl.ds(start, side)])
-    y = mm3((row_ref[0], row_ref[1]), slab)
-    out_ref[...] = as_spectrum(mm3(split(y), (edge_ref[focus, 0], edge_ref[focus, 1])))
+    start = pl.multiple_of((1 - focus) * (mask_hbm.shape[1] - side), 128)
+    sends = out_ref.shape[0]
+    copies = [
+        pltpu.make_async_copy(pupil_hbm.at[:, :, corner_of(d)], pupil_ref.at[d], sems.at[4 + d])
+        for d in range(sends)
+    ]
+    copies += [
+        pltpu.make_async_copy(weights_hbm, weights_ref, sems.at[0]),
+        pltpu.make_async_copy(mask_hbm.at[:, pl.ds(start, side)], mask_ref, sems.at[1]),
+        pltpu.make_async_copy(row_hbm, row_ref, sems.at[2]),
+        pltpu.make_async_copy(edge_hbm.at[focus], table_ref, sems.at[3]),
+    ]
+    for copy in copies:
+        copy.start()
+    for copy in copies:
+        copy.wait()
+    for d in range(sends):
+        for s in range(out_ref.shape[1]):
+            scale = source_scale(weights_ref, s, sources)
+            re, im = (pupil_ref[d, c, s] * scale for c in range(2))
+            out_ref[d, s] = jnp.concatenate([re, im], axis=1)
+    y = mm3((row_ref[0], row_ref[1]), split(mask_ref[...]))
+    edge_ref[...] = as_spectrum(mm3(split(y), (table_ref[0], table_ref[1])))
 
 
 def own_kernel(
@@ -267,6 +303,12 @@
     return jnp.where(low, t1 + swapped_halves(t1), t2 - swapped_halves(t2))
 
 
+def fetch(counts_hbm, counts_ref, sem):
+    copy = pltpu.make_async_copy(counts_hbm, counts_ref, sem)
+    copy.start()
+    return copy
+
+
 def active_here(corner_of, counts_ref):
     used = counts_ref[lax.axis_index("tile")]
     return (corner_of() < used).astype(jnp.float32)
@@ -278,16 +320,18 @@
     return lambda pair, half: packs[half][pair]
 
 
-def main_kernel(n_spec, n_pack, corner_of, counts_ref, *refs):
+def main_kernel(n_spec, n_pack, corner_of, counts_hbm, *refs):
     specs, refs = refs[:n_spec], refs[n_spec:]
     packs, refs = refs[:n_pack], refs[n_pack:]
     target_ref, right1_ref, left2_ref, right1t_ref, back2_ref, up_ref, upt_ref = refs[:7]
-    out_ref, field_ref, data_ref, rows_ref = refs[7:]
+    out_ref, field_ref, data_ref, rows_ref, counts_ref, sem = refs[7:]
+    copy = fetch(counts_hbm, counts_ref, sem)
     spec = sum(ref[...] for ref in specs[1:]) + specs[0][...]
     pupil_of = pick(packs)
     count = n_pack * packs[0].shape[0] // 2
     work = (field_ref, data_ref, rows_ref)
     intensity = forward(spec, pupil_of, count, pair_of(right1_ref), left2_ref, *work)
+    copy.wait()
     out_ref[...] = adjoint(
         intensity,
         target_ref[...],
@@ -317,11 +361,12 @@
     )
 
 
-def adjoint_kernel(n_part, n_pack, corner_of, counts_ref, *refs):
+def adjoint_kernel(n_part, n_pack, corner_of, counts_hbm, *refs):
     parts, refs = refs[:n_part], refs[n_part:]
     packs, refs = refs[:n_pack], refs[n_pack:]
     target_ref, right1t_ref, back2_ref, up_ref, upt_ref, field_ref = refs[:6]
-    out_ref, data_ref, rows_ref = refs[6:]
+    out_ref, data_ref, rows_ref, counts_ref, sem = refs[6:]
+    fetch(counts_hbm, counts_ref, sem).wait()
     out_ref[...] = adjoint(
         sum(ref[...] for ref in parts[1:]) + parts[0][...],
         target_ref[...],
@@ -338,33 +383,31 @@
     )
 
 
-def final_kernel(n_own, n_near, *refs):
-    own, refs = refs[:n_own], refs[n_own:]
-    near, refs = refs[:n_near], refs[n_near:]
-    across_ref, rowt_ref, colown_ref, coledge_ref, out_ref = refs
+def lines(gs, rowt_ref, rows):
+    strip = lax.axis_index("src") * lax.axis_size("focus") + lax.axis_index("focus")
+    start = pl.multiple_of(strip * rows, rows)
+    rowt = (rowt_ref[0, pl.ds(start, rows)], rowt_ref[1, pl.ds(start, rows)])
+    turned = swapped_halves(gs)
+    stack = jnp.concatenate([gs, jnp.where(left_lanes(gs.shape), turned, -turned)], axis=0)
+    return split(mm3(rowt, split(stack)))
+
+
+def middle_kernel(gs_ref, rowt_ref, colown_ref, out_ref):
+    out_ref[...] = mm3(
+        lines(gs_ref[...], rowt_ref, out_ref.shape[0]), (colown_ref[0], colown_ref[1])
+    )
+
+
+def border_kernel(which_of, base_ref, gs_ref, rowt_ref, coledge_ref, out_ref):
     rows, tile = out_ref.shape
     side = coledge_ref.shape[3]
-    focus = lax.axis_index("focus")
-    strip = lax.axis_index("src") * lax.axis_size("focus") + focus
-    start = pl.multiple_of(strip * rows, rows)
-    rowt = (rowt_ref[0, pl.ds(start, rows)], rowt_ref[1, pl.ds(start, rows)])
-
-    def lines(gs):
-        turned = swapped_halves(gs)
-        stack = jnp.concatenate([gs, jnp.where(left_lanes(gs.shape), turned, -turned)], axis=0)
-        return split(mm3(rowt, split(stack)))
-
-    received = sum(ref[...] for ref in near[1:]) + near[0][...]
-    across = across_ref[...]
-    first = focus == 0
-    from_right = jnp.where(first, received, across)
-    from_left = jnp.where(first, across, received)
-    main = mm3(lines(sum(ref[...] for ref in own[1:]) + own[0][...]), (colown_ref[0], colown_ref[1]))
-    high = mm3(lines(from_right), (coledge_ref[0, 0], coledge_ref[0, 1]))
-    low = mm3(lines(from_left), (coledge_ref[1, 0], coledge_ref[1, 1]))
-    out_ref[...] = main
-    out_ref[:, :side] = out_ref[:, :side] + low
-    out_ref[:, tile - side :] = out_ref[:, tile - side :] + high
+    which = which_of()
+    part = mm3(
+        lines(gs_ref[...], rowt_ref, rows), (coledge_ref[which, 0], coledge_ref[which, 1])
+    )
+    out_ref[...] = base_ref[...]
+    at = pl.ds(pl.multiple_of((1 - which) * (tile - side), 128), side)
+    out_ref[:, at] = out_ref[:, at] + part
 
 
 def call(kernel, shapes, specs, scratch=(), flops=0, limit=8):
@@ -382,6 +425,10 @@
     )
 
 
+def in_hbm(x):
+    return pltpu.with_memory_space_constraint(x, pltpu.HBM)
+
+
 class Shape:
     def __init__(self, *shape):
         self.shape = shape
@@ -432,17 +479,22 @@
                 pairs.append((place(t + 1, s, 1), place(t, u, 0)))
         return lax.ppermute(value, ("tile", "src", "focus"), pairs)
 
-    got = []
-    if group > 1:
-        sends = call(
-            lambda *refs: send_kernel(sources, lambda d: group_corner(d + 1), *refs),
-            Shape(group - 1, local_src, freqs, 2 * freqs),
-            [SMEM, VMEM],
-        )(weights, pupil)
-        got = [hop_group(sends[d - 1], d) for d in range(1, group)]
-    edge = call(edge_kernel, Shape(freqs, 2 * freqs), [VMEM, VMEM, VMEM])(
-        mask, tables["row"], tables["edge"]
-    )
+    sends = group - 1
+    side = tables["edge"].shape[2]
+    edge, sent = call(
+        lambda *refs: first_kernel(sources, lambda d: group_corner(d + 1), *refs),
+        [(freqs, 2 * freqs), (max(sends, 1), local_src, freqs, 2 * freqs)],
+        [HBM] * 5,
+        [
+            pltpu.SMEM(weights.shape, jnp.float32),
+            pltpu.VMEM((max(sends, 1), 2, local_src, freqs, freqs), jnp.float32),
+            pltpu.VMEM((tile, side), jnp.float32),
+            pltpu.VMEM(tables["row"].shape, jnp.bfloat16),
+            pltpu.VMEM(tables["edge"].shape[1:], jnp.bfloat16),
+            pltpu.SemaphoreType.DMA((4 + max(sends, 1),)),
+        ],
+    )(*(in_hbm(x) for x in (weights, pupil, mask, tables["row"], tables["edge"])))
+    got = [hop_group(sent[d - 1], d) for d in range(1, group)]
     near = hop_tile(edge, 0)
     spec, own_pack = call(
         lambda *refs: own_kernel(sources, group_corner, *refs),
@@ -450,6 +502,7 @@
         [SMEM, VMEM, VMEM, VMEM, VMEM],
         flops=10**9,
     )(weights, pupil, mask, tables["row"], tables["colt"])
+    near, spec, own_pack = lax.optimization_barrier((near, spec, own_pack))
     specs = [spec, near, hop_focus(near)]
 
     gradient = []
@@ -478,15 +531,16 @@
             pltpu.VMEM((count // 2, 2 * grid, 2 * grid), jnp.bfloat16),
             pltpu.VMEM((count, grid, 2 * grid), jnp.bfloat16),
         ]
+        used = [pltpu.SMEM(counts.shape, jnp.int32), pltpu.SemaphoreType.DMA]
         before, after = ("right1", "left2"), ("right1t", "back2", "up", "upt")
         if n_src == group:
             gs = call(
                 lambda *refs: main_kernel(len(specs), n_pack, corner_of, *refs),
                 Shape(freqs, 2 * freqs),
-                [SMEM] + [VMEM] * (len(specs) + n_pack + 7),
-                [pltpu.VMEM(field, jnp.float32)] + work,
+                [HBM] + [VMEM] * (len(specs) + n_pack + 7),
+                [pltpu.VMEM(field, jnp.float32)] + work + used,
                 limit=24,
-            )(counts, *specs, *packs, target, *(tables[k] for k in before + after))
+            )(in_hbm(counts), *specs, *packs, target, *(tables[k] for k in before + after))
         else:
             part, fields = call(
                 lambda *refs: forward_kernel(len(specs), n_pack, *refs),
@@ -499,22 +553,33 @@
             gs = call(
                 lambda *refs: adjoint_kernel(len(parts), n_pack, corner_of, *refs),
                 Shape(freqs, 2 * freqs),
-                [SMEM] + [VMEM] * (len(parts) + n_pack + 6),
-                work,
+                [HBM] + [VMEM] * (len(parts) + n_pack + 6),
+                work + used,
                 limit=24,
-            )(counts, *parts, *packs, target, *(tables[k] for k in after), fields)
+            )(in_hbm(counts), *parts, *packs, target, *(tables[k] for k in after), fields)
         gradient.append(gs)
     gs = sum(gradient[1:]) + gradient[0] if len(gradient) > 1 else gradient[0]
     gs = gs + hop_focus(gs)
     gs = sum([hop_src(gs, d) for d in range(1, n_src)], gs)
+    rows = tile // (n_src * n_focus)
     received = hop_tile(gs, 0)
+    out = call(middle_kernel, Shape(rows, tile), [VMEM] * 3, flops=10**9)(
+        gs, tables["rowt"], tables["colown"]
+    )
+    received, out = lax.optimization_barrier((received, out))
     across = hop_focus(received)
-    rows = tile // (n_src * n_focus)
+    out = call(
+        lambda *refs: border_kernel(lambda: lax.axis_index("focus"), *refs),
+        Shape(rows, tile),
+        [VMEM] * 4,
+        flops=10**9,
+    )(out, received, tables["rowt"], tables["coledge"])
+    across, out = lax.optimization_barrier((across, out))
     return call(
-        lambda *refs: final_kernel(1, 1, *refs),
+        lambda *refs: border_kernel(lambda: 1 - lax.axis_index("focus"), *refs),
         Shape(rows, tile),
-        [VMEM] * 6,
-    )(gs, received, across, *(tables[k] for k in ("rowt", "colown", "coledge")))
+        [VMEM] * 4,
+    )(out, across, tables["rowt"], tables["coledge"])
 
 
 def solution(mesh):

time: 33.1 us -> 28.5 us (0.86)
  local copies, waits for them, and re-layouts: 4.51 us -> 0.98 us
  waiting for transfers between devices: 11.4 us -> 8.73 us
  starting transfers between devices: 8.81 us -> 9.73 us
  Pallas kernels: 7.97 us -> 8.63 us
    unnamed x36 -> x28, local copies, waits for them, and re-layouts: 4.51 us -> 0.98 us
    ppermute x2, waiting for transfers between devices: 5.52 us -> 3.17 us  [hop_tile(): return lax.ppermute(value, ('tile', 'src', 'focus'), pairs)]
    ppermute x1, starting transfers between devices: 0.17 us -> 1.46 us  [hop_src(): lax.ppermute(value, 'src', [(i, (i + by) % n_src) for i in range(n_src)])]
    ppermute x1, waiting for transfers between devices: 3.75 us -> 2.45 us  [hop_src(): lax.ppermute(value, 'src', [(i, (i + by) % n_src) for i in range(n_src)])]
    pallas_call x3 -> x4, Pallas kernels: 2.38 us -> 3.54 us  [the longest x1 1.78 us: per_device(): call(lambda *refs: first_kernel(sources, lambda d: group_corner(d + 1), *...]
    ppermute x3, waiting for transfers between devices: 2.09 us -> 3.1 us  [hop_focus(): return lax.ppermute(value, 'focus', [(0, 1), (1, 0)])]
    pallas_call x1, Pallas kernels: 4.45 us -> 3.95 us  [per_device(): call(lambda *refs: main_kernel(len(specs), n_pack, corner_of, *refs), Sha...]
    ppermute x3, starting transfers between devices: 0.55 us -> 0.22 us  [hop_focus(): return lax.ppermute(value, 'focus', [(0, 1), (1, 0)])]
  transfers between devices with their start and end apart: 7 -> 7, of which waited for: 5 -> 6; matrix products, arithmetic and copies ran while one was open for 0% -> 0% of each run, Pallas kernels for 5% -> 7%
where the time goes in v4:
time: 28.5 us; the launch traced here: 28.3 us
  starting transfers between devices  9.73 us (34%)
  waiting for transfers between devices  8.73 us (31%)
  Pallas kernels  8.63 us (30%)
  local copies, waits for them, and re-layouts  0.98 us (3%)
    ppermute x2, starting transfers between devices, hop_tile(): return lax.ppermute(value, ('tile', 'src', 'focus'), pairs)  4.99 us
    pallas_call x1, Pallas kernels, per_device(): call(lambda *refs: main_kernel(len(specs), n_pack, corner_of, *refs), Sha...  3.95 us
    ppermute x2, waiting for transfers between devices, hop_tile(): return lax.ppermute(value, ('tile', 'src', 'focus'), pairs)  3.17 us
    ppermute x3, waiting for transfers between devices, hop_focus(): return lax.ppermute(value, 'focus', [(0, 1), (1, 0)])  3.1 us
    ppermute x1, starting transfers between devices, hop_group(): return lax.ppermute(value, 'src', pairs)  3.05 us
    ppermute x1, waiting for transfers between devices, hop_src(): lax.ppermute(value, 'src', [(i, (i + by) % n_src) for i in range(n_src)])  2.45 us
    pallas_call x1, Pallas kernels, per_device(): call(lambda *refs: first_kernel(sources, lambda d: group_corner(d + 1), *...  1.78 us
    ppermute x1, starting transfers between devices, hop_src(): lax.ppermute(value, 'src', [(i, (i + by) % n_src) for i in range(n_src)])  1.46 us
  transfers between devices with their start and end apart: 7, of which 6 were waited for; matrix products, arithmetic and copies ran while one was open for 0% of the time, Pallas kernels for 7%

profile of v4, /device:TPU:0, one launch (start us, length us, event | category | flops | bytes accessed | tf_op | source)
XLA Modules:
  0.0 28.3 jit_solution(12904034053333082537)
XLA Ops:
  0.0 1.8 %shard_map.163 = (f32[64,128]{1,0:T(8,128)S(1)}, f32[1,8,64,128]{3,2,1,0:T(8,128)S(1)}) custom-call(f32[8]{0:T(128)} %refs_0_.4, f32[2,8,2,64,64]{4,3,2,1,0:T(8,128)} %refs_1_.3, f32[384,384]{1,0:T(8,128)} %refs_2_.5, bf16[2,128,384]{2,1,0:T(8,128)(2,1)} %constant.20.clone.refs_3_.colown_ref, bf16[2,2,128,128]{3,2,1,0:T(8,128)(2,1)} %constant.22.clone.refs_4_), custom_call_target="tpu_custom_call" | custom-call | bytes 1048576 | tf_op jit(solution)/shard_map/pallas_call | solution.py:484
  1.8 0.0 copy-start.13
  1.8 3.0 %collective-permute-start.2 = (f32[8,64,128]{2,1,0:T(8,128)S(1)}, f32[8,64,128]{2,1,0:T(8,128)S(1)}, u32[]{:S(2)}, u32[]{:S(2)}) collective-permute-start(f32[8,64,128]{2,1,0:T(8,128)S(1)} %bitcast.1), channel_id=1, source_target_pairs={{0,2},{2,0},{1,3},{3,1},{4,6},{6,4},{5,7},{7,5},{8,10},{10,8},{9,1... | collective-permute-start | bytes 786440 | tf_op jit(solution)/shard_map/ppermute | solution.py:465
  4.9 2.8 %collective-permute-start = (f32[64,128]{1,0:T(8,128)S(1)}, f32[64,128]{1,0:T(8,128)S(1)}, u32[]{:S(2)}, u32[]{:S(2)}) collective-permute-start(f32[64,128]{1,0:T(8,128)S(1)} %get-tuple-element.16), channel_id=1, source_target_pairs={{0,5},{5,0},{2,7},{7,2},{4,9},{9,4},{6,11},{11,6},{8,13},{13,8},{1... | collective-permute-start | bytes 98312 | tf_op jit(solution)/shard_map/ppermute | solution.py:480
  7.7 0.0 copy-start.6
  7.7 0.9 %copy-done.6 = bf16[2,384,128]{2,1,0:T(8,128)(2,1)S(1)} copy-done((bf16[2,384,128]{2,1,0:T(8,128)(2,1)S(1)}, bf16[2,384,128]{2,1,0:T(8,128)(2,1)}, u32[]{:S(2)}) %copy-start.6) | copy-done | bytes 196632
  8.6 1.1 %shard_map.164 = (f32[64,128]{1,0:T(8,128)S(1)}, f32[8,64,128]{2,1,0:T(8,128)S(1)}) custom-call(f32[8]{0:T(128)S(1)} %copy-done.13, f32[2,8,2,64,64]{4,3,2,1,0:T(8,128)S(1)} %copy-done, f32[384,384]{1,0:T(8,128)S(1)} %copy-done.2, bf16[2,128,384]{2,1,0:T(8,128)(2,1)S(1)} %copy-done.3, bf16[2,384,128]{2,1,0:T(8,128)(2,1)S(1)} %copy-done.6), custom_call_target="tpu_custom_call" | custom-call | flops 1000000000 | bytes 1048576 | tf_op jit(solution)/shard_map/pallas_call | solution.py:499
  9.8 0.5 %collective-permute-done.refs_2_ = f32[64,128]{1,0:T(8,128)S(1)} collective-permute-done((f32[64,128]{1,0:T(8,128)S(1)}, f32[64,128]{1,0:T(8,128)S(1)}, u32[]{:S(2)}, u32[]{:S(2)}) %collective-permute-start) | collective-permute-done | bytes 32800 | tf_op jit(solution)/shard_map/ppermute | solution.py:480
  10.2 0.0 collective-permute-start.1
  10.2 1.2 %collective-permute-done.1.refs_3_ = f32[64,128]{1,0:T(8,128)S(1)} collective-permute-done((f32[64,128]{1,0:T(8,128)S(1)}, f32[64,128]{1,0:T(8,128)S(1)}, u32[]{:S(2)}, u32[]{:S(2)}) %collective-permute-start.1) | collective-permute-done | bytes 32800 | tf_op jit(solution)/shard_map/ppermute | solution.py:468
  11.4 0.0 collective-permute-done.2.refs_5_
  11.5 4.0 %shard_map.165 = f32[64,128]{1,0:T(8,128)S(1)} custom-call(s32[4]{0:T(128)} %refs_0_.5, f32[64,128]{1,0:T(8,128)S(1)} %get-tuple-element.19.refs_1_, f32[64,128]{1,0:T(8,128)S(1)} %collective-permute-done.refs_2_, f32[64,128]{1,0:T(8,128)S(1)} %collective-permute-done.1.refs_3_, f32[8,64,128]{2,1,0:T(8,128)S(1)} %get-tuple-element.21.refs_4_, ...), custom_call_target="tpu_custom_call" | custom-call | bytes 1048576 | tf_op jit(solution)/shard_map/pallas_call | solution.py:537
  15.4 0.0 copy-start.7
  15.5 0.2 collective-permute-start.3
  15.7 1.1 %collective-permute-done.3 = f32[64,128]{1,0:T(8,128)S(1)} collective-permute-done((f32[64,128]{1,0:T(8,128)S(1)}, f32[64,128]{1,0:T(8,128)S(1)}, u32[]{:S(2)}, u32[]{:S(2)}) %collective-permute-start.3) | collective-permute-done | bytes 32800 | tf_op jit(solution)/shard_map/ppermute | solution.py:468
  16.7 1.5 %collective-permute-start.4 = (f32[64,128]{1,0:T(8,128)S(1)}, f32[64,128]{1,0:T(8,128)S(1)}, u32[]{:S(2)}, u32[]{:S(2)}) collective-permute-start(f32[64,128]{1,0:T(8,128)S(1)} %add.6), channel_id=1, source_target_pairs={{0,2},{2,0},{1,3},{3,1},{4,6},{6,4},{5,7},{7,5},{8,10},{10,8},{9,1... | collective-permute-start | bytes 98312 | tf_op jit(solution)/shard_map/ppermute | solution.py:461
  18.2 2.5 %collective-permute-done.4 = f32[64,128]{1,0:T(8,128)S(1)} collective-permute-done((f32[64,128]{1,0:T(8,128)S(1)}, f32[64,128]{1,0:T(8,128)S(1)}, u32[]{:S(2)}, u32[]{:S(2)}) %collective-permute-start.4) | collective-permute-done | bytes 32800 | tf_op jit(solution)/shard_map/ppermute | solution.py:461
  20.7 2.2 %collective-permute-start.5 = (f32[64,128]{1,0:T(8,128)S(1)}, f32[64,128]{1,0:T(8,128)S(1)}, u32[]{:S(2)}, u32[]{:S(2)}) collective-permute-start(f32[64,128]{1,0:T(8,128)S(1)} %add.7.gs_ref), channel_id=1, source_target_pairs={{0,5},{5,0},{2,7},{7,2},{4,9},{9,4},{6,11},{11,6},{8,13},{13,8},{1... | collective-permute-start | bytes 98312 | tf_op jit(solution)/shard_map/ppermute | solution.py:480
  22.9 0.4 %shard_map.166.refs_0_ = f32[96,384]{1,0:T(8,128)S(1)} custom-call(f32[64,128]{1,0:T(8,128)S(1)} %add.7.gs_ref, bf16[2,384,128]{2,1,0:T(8,128)(2,1)S(1)} %copy-done.7, bf16[2,128,384]{2,1,0:T(8,128)(2,1)S(1)} %copy-done.3), custom_call_target="tpu_custom_call" | custom-call | flops 1000000000 | bytes 1048576 | tf_op jit(solution)/shard_map/pallas_call | solution.py:566
  23.3 2.7 %collective-permute-done.5.refs_1_ = f32[64,128]{1,0:T(8,128)S(1)} collective-permute-done((f32[64,128]{1,0:T(8,128)S(1)}, f32[64,128]{1,0:T(8,128)S(1)}, u32[]{:S(2)}, u32[]{:S(2)}) %collective-permute-start.5) | collective-permute-done | bytes 32800 | tf_op jit(solution)/shard_map/ppermute | solution.py:480
  26.0 0.0 collective-permute-start.6
  26.0 0.4 %shard_map.167.refs_0_ = f32[96,384]{1,0:T(8,128)S(1)} custom-call(f32[96,384]{1,0:T(8,128)S(1)} %shard_map.166.refs_0_, f32[64,128]{1,0:T(8,128)S(1)} %collective-permute-done.5.refs_1_, bf16[2,384,128]{2,1,0:T(8,128)(2,1)S(1)} %copy-done.7, bf16[2,2,128,128]{3,2,1,0:T(8,128)(2,1)S(1)} %copy-done.8), custom_call_target="tpu_custom_call" | custom-call | flops 1000000000 | bytes 1048576 | tf_op jit(solution)/shard_map/pallas_call | solution.py:571
  26.4 0.8 %collective-permute-done.6.refs_1_ = f32[64,128]{1,0:T(8,128)S(1)} collective-permute-done((f32[64,128]{1,0:T(8,128)S(1)}, f32[64,128]{1,0:T(8,128)S(1)}, u32[]{:S(2)}, u32[]{:S(2)}) %collective-permute-start.6) | collective-permute-done | bytes 32800 | tf_op jit(solution)/shard_map/ppermute | solution.py:468
  27.2 1.0 %shard_map.168 = f32[96,384]{1,0:T(8,128)} custom-call(f32[96,384]{1,0:T(8,128)S(1)} %shard_map.167.refs_0_, f32[64,128]{1,0:T(8,128)S(1)} %collective-permute-done.6.refs_1_, bf16[2,384,128]{2,1,0:T(8,128)(2,1)S(1)} %copy-done.7, bf16[2,2,128,128]{3,2,1,0:T(8,128)(2,1)S(1)} %copy-done.8), custom_call_target="tpu_custom_call" | custom-call | bytes 1048576 | tf_op jit(solution)/shard_map/pallas_call | solution.py:578
  (26 shorter events, 0.1 us)
Async XLA Ops:
  0.0 7.6 %copy-start.3 = (bf16[2,128,384]{2,1,0:T(8,128)(2,1)S(1)}, bf16[2,128,384]{2,1,0:T(8,128)(2,1)}, u32[]{:S(2)}) copy-start(bf16[2,128,384]{2,1,0:T(8,128)(2,1)} %constant.20.clone.refs_3_.colown_ref) | copy-start | bytes 589828
  0.0 7.6 %copy-start = (f32[2,8,2,64,64]{4,3,2,1,0:T(8,128)S(1)}, f32[2,8,2,64,64]{4,3,2,1,0:T(8,128)}, u32[]{:S(2)}) copy-start(f32[2,8,2,64,64]{4,3,2,1,0:T(8,128)} %refs_1_.3) | copy-start | bytes 1572868
  0.0 7.7 %copy-start.2 = (f32[384,384]{1,0:T(8,128)S(1)}, f32[384,384]{1,0:T(8,128)}, u32[]{:S(2)}) copy-start(f32[384,384]{1,0:T(8,128)} %refs_2_.5) | copy-start | bytes 1769476
  1.8 5.9 %copy-start.13 = (f32[8]{0:T(128)S(1)}, f32[8]{0:T(128)}, u32[]{:S(2)}) copy-start(f32[8]{0:T(128)} %refs_0_.4) | copy-start | bytes 100
  1.8 9.6 %collective-permute-start.2 = (f32[8,64,128]{2,1,0:T(8,128)S(1)}, f32[8,64,128]{2,1,0:T(8,128)S(1)}, u32[]{:S(2)}, u32[]{:S(2)}) collective-permute-start(f32[8,64,128]{2,1,0:T(8,128)S(1)} %bitcast.1), channel_id=1, source_target_pairs={{0,2},{2,0},{1,3},{3,1},{4,6},{6,4},{5,7},{7,5},{8,10},{10,8},{9,1... | collective-permute-start | bytes 786440 | tf_op jit(solution)/shard_map/ppermute | solution.py:465
  4.9 6.6 %copy-start.1 = (f32[384,384]{1,0:T(8,128)S(1)}, f32[384,384]{1,0:T(8,128)}, u32[]{:S(2)}) copy-start(f32[384,384]{1,0:T(8,128)} %refs_6_.1) | copy-start | bytes 1769476
  4.9 6.6 %copy-start.4 = (bf16[2,128,384]{2,1,0:T(8,128)(2,1)S(1)}, bf16[2,128,384]{2,1,0:T(8,128)(2,1)}, u32[]{:S(2)}) copy-start(bf16[2,128,384]{2,1,0:T(8,128)(2,1)} %constant.27.clone.refs_12_) | copy-start | bytes 589828
  4.9 6.6 %copy-start.5 = (bf16[2,384,128]{2,1,0:T(8,128)(2,1)S(1)}, bf16[2,384,128]{2,1,0:T(8,128)(2,1)}, u32[]{:S(2)}) copy-start(bf16[2,384,128]{2,1,0:T(8,128)(2,1)} %constant.26.clone.refs_11_) | copy-start | bytes 589828
  4.9 5.4 %collective-permute-start = (f32[64,128]{1,0:T(8,128)S(1)}, f32[64,128]{1,0:T(8,128)S(1)}, u32[]{:S(2)}, u32[]{:S(2)}) collective-permute-start(f32[64,128]{1,0:T(8,128)S(1)} %get-tuple-element.16), channel_id=1, source_target_pairs={{0,5},{5,0},{2,7},{7,2},{4,9},{9,4},{6,11},{11,6},{8,13},{13,8},{1... | collective-permute-start | bytes 98312 | tf_op jit(solution)/shard_map/ppermute | solution.py:480
  7.7 0.9 %copy-start.6 = (bf16[2,384,128]{2,1,0:T(8,128)(2,1)S(1)}, bf16[2,384,128]{2,1,0:T(8,128)(2,1)}, u32[]{:S(2)}) copy-start(bf16[2,384,128]{2,1,0:T(8,128)(2,1)} %constant.21.clone.refs_4_.rowt_ref.refs_2_) | copy-start | bytes 589828
  8.6 2.8 %copy-start.9 = (bf16[2,256,128]{2,1,0:T(8,128)(2,1)S(1)}, bf16[2,256,128]{2,1,0:T(8,128)(2,1)}, u32[]{:S(2)}) copy-start(bf16[2,256,128]{2,1,0:T(8,128)(2,1)} %constant.29.clone.refs_9_) | copy-start | bytes 393220
  8.6 2.9 %copy-start.10 = (bf16[256,256]{1,0:T(8,128)(2,1)S(1)}, bf16[256,256]{1,0:T(8,128)(2,1)}, u32[]{:S(2)}) copy-start(bf16[256,256]{1,0:T(8,128)(2,1)} %constant.25.clone.refs_10_) | copy-start | bytes 393220
  8.6 2.9 %copy-start.11 = (bf16[256,192]{1,0:T(8,128)(2,1)S(1)}, bf16[256,192]{1,0:T(8,128)(2,1)}, u32[]{:S(2)}) copy-start(bf16[256,192]{1,0:T(8,128)(2,1)} %constant.24.clone.refs_8_) | copy-start | bytes 294916
  8.6 2.9 %copy-start.12 = (bf16[2,128,256]{2,1,0:T(8,128)(2,1)S(1)}, bf16[2,128,256]{2,1,0:T(8,128)(2,1)}, u32[]{:S(2)}) copy-start(bf16[2,128,256]{2,1,0:T(8,128)(2,1)} %constant.23.clone.refs_7_) | copy-start | bytes 393220
  10.2 1.2 %collective-permute-start.1 = (f32[64,128]{1,0:T(8,128)S(1)}, f32[64,128]{1,0:T(8,128)S(1)}, u32[]{:S(2)}, u32[]{:S(2)}) collective-permute-start(f32[64,128]{1,0:T(8,128)S(1)} %collective-permute-done.refs_2_), channel_id=1, source_target_pairs={{0,1},{1,0},{2,3},{3,2},{4,5},{5,4},{6,7},{7,6},{8,9},{9,8},{10,11... | collective-permute-start | bytes 98312 | tf_op jit(solution)/shard_map/ppermute | solution.py:468
  15.4 7.5 %copy-start.7 = (bf16[2,384,128]{2,1,0:T(8,128)(2,1)S(1)}, bf16[2,384,128]{2,1,0:T(8,128)(2,1)}, u32[]{:S(2)}) copy-start(bf16[2,384,128]{2,1,0:T(8,128)(2,1)} %constant.21.clone.refs_4_.rowt_ref.refs_2_) | copy-start | bytes 589828
  15.5 1.3 %collective-permute-start.3 = (f32[64,128]{1,0:T(8,128)S(1)}, f32[64,128]{1,0:T(8,128)S(1)}, u32[]{:S(2)}, u32[]{:S(2)}) collective-permute-start(f32[64,128]{1,0:T(8,128)S(1)} %shard_map.165), channel_id=1, source_target_pairs={{0,1},{1,0},{2,3},{3,2},{4,5},{5,4},{6,7},{7,6},{8,9},{9,8},{10,11... | collective-permute-start | bytes 98312 | tf_op jit(solution)/shard_map/ppermute | solution.py:468
  16.7 3.9 %collective-permute-start.4 = (f32[64,128]{1,0:T(8,128)S(1)}, f32[64,128]{1,0:T(8,128)S(1)}, u32[]{:S(2)}, u32[]{:S(2)}) collective-permute-start(f32[64,128]{1,0:T(8,128)S(1)} %add.6), channel_id=1, source_target_pairs={{0,2},{2,0},{1,3},{3,1},{4,6},{6,4},{5,7},{7,5},{8,10},{10,8},{9,1... | collective-permute-start | bytes 98312 | tf_op jit(solution)/shard_map/ppermute | solution.py:461
  20.7 5.4 %copy-start.8 = (bf16[2,2,128,128]{3,2,1,0:T(8,128)(2,1)S(1)}, bf16[2,2,128,128]{3,2,1,0:T(8,128)(2,1)}, u32[]{:S(2)}) copy-start(bf16[2,2,128,128]{3,2,1,0:T(8,128)(2,1)} %constant.28.clone.refs_3_) | copy-start | bytes 393220
  20.7 5.4 %collective-permute-start.5 = (f32[64,128]{1,0:T(8,128)S(1)}, f32[64,128]{1,0:T(8,128)S(1)}, u32[]{:S(2)}, u32[]{:S(2)}) collective-permute-start(f32[64,128]{1,0:T(8,128)S(1)} %add.7.gs_ref), channel_id=1, source_target_pairs={{0,5},{5,0},{2,7},{7,2},{4,9},{9,4},{6,11},{11,6},{8,13},{13,8},{1... | collective-permute-start | bytes 98312 | tf_op jit(solution)/shard_map/ppermute | solution.py:480
  26.0 1.2 %collective-permute-start.6 = (f32[64,128]{1,0:T(8,128)S(1)}, f32[64,128]{1,0:T(8,128)S(1)}, u32[]{:S(2)}, u32[]{:S(2)}) collective-permute-start(f32[64,128]{1,0:T(8,128)S(1)} %collective-permute-done.5.refs_1_), channel_id=1, source_target_pairs={{0,1},{1,0},{2,3},{3,2},{4,5},{5,4},{6,7},{7,6},{8,9},{9,8},{10,11... | collective-permute-start | bytes 98312 | tf_op jit(solution)/shard_map/ppermute | solution.py:468
